TPU v7x, 512 devices: a whole 4x4x16 slice. The times are simulated.
512 devices in a mesh: fsdp: 64 (over y_lo, z, core), expert: 8 (over y_hi, x).
Axes of the slice: x: 4, y: 4 (y_hi: 2, y_lo: 2; y = y_hi * 2 + y_lo), z: 16, core: 2. Of those that a mesh axis runs over, the one named last changes fastest.
Arguments:
- tokens: bfloat16 [8192, 5120], P('expert', 'fsdp'), may hold values from -6 to 6
- out_grad: bfloat16 [8192, 5120], P('expert', 'fsdp'), may hold values from -6 to 6
- slot_rows: int32 [8, 8, 24], P('expert'), may hold values from 0 to 1023, as said below
- expert_counts: int32 [8, 8], P('expert'), may hold values from 1 to 24, as said below
- route_prob: float32 [8, 192], P('expert'), may hold values from 0.05 to 0.9
- w_gate: bfloat16 [8, 5120, 1536], P('expert', 'fsdp'), may hold values from -0.078125 to 0.078125
- w_up: bfloat16 [8, 5120, 1536], P('expert', 'fsdp'), may hold values from -0.078125 to 0.078125
- w_down: bfloat16 [8, 5120, 1536], P('expert', 'fsdp'), may hold values from -0.15625 to 0.15625
Outputs:
- token_grad: bfloat16 [8192, 5120], P('expert', 'fsdp')
- gate_grad: float32 [8, 5120, 1536], P('expert', 'fsdp')
- up_grad: float32 [8, 5120, 1536], P('expert', 'fsdp')
- down_grad: float32 [8, 5120, 1536], P('expert', 'fsdp')
- prob_grad: float32 [8, 192], P('expert', 'fsdp')
Inputs may be any that keep to these rules, and one draw needn't show every extreme that they name: `slot_rows`: for each token group and expert the 24 listed rows are distinct. `expert_counts`: in every draw one expert has all 24 slots live from every token group.
All inputs are finite; a program needn't handle non-finite values.
Results may differ from a plain program's by a relative error of at most 0.0055.
Values may be sent and summed in bfloat16 or wider, within the bound.
A program may use at most 64 MiB of HBM per device.

v0:
```python
import jax
import jax.numpy as jnp
from jax import lax
from jax.sharding import PartitionSpec as P


def hidden_backward(gate_sum, up_sum, down_sum, row_prob, live_mask):
    sigmoid_gate = jax.nn.sigmoid(gate_sum)
    silu_gate = gate_sum * sigmoid_gate
    hidden = lax.optimization_barrier((silu_gate * up_sum).astype(jnp.bfloat16)).astype(jnp.float32)
    row_scale = (row_prob * live_mask)[:, None]
    scaled_hidden = (hidden * row_scale).astype(jnp.bfloat16)
    hidden_grad = down_sum * row_scale
    up_act_grad = (hidden_grad * silu_gate).astype(jnp.bfloat16)
    gate_act_grad = (
        hidden_grad * up_sum * sigmoid_gate * (1.0 + gate_sum * (1.0 - sigmoid_gate))
    ).astype(jnp.bfloat16)
    prob_grad = live_mask * jnp.sum(hidden * down_sum, axis=1)
    return (scaled_hidden, gate_act_grad, up_act_grad, prob_grad)


def local(tokens, out_grad, slot_rows, expert_counts, route_prob, w_gate, w_up, w_down):
    sent_rows = slot_rows[0]
    recv_tokens, recv_grads = (
        lax.all_to_all(tokens[sent_rows], "expert", split_axis=0, concat_axis=0, tiled=True),
        lax.all_to_all(out_grad[sent_rows], "expert", split_axis=0, concat_axis=0, tiled=True),
    )
    source_count, slot_count, feature_count = recv_tokens.shape
    total_rows = source_count * slot_count
    token_rows = recv_tokens.reshape(total_rows, feature_count)
    grad_rows = recv_grads.reshape(total_rows, feature_count)
    live_mask = (
        (jnp.arange(slot_count, dtype=jnp.int32)[None, :] < expert_counts[0][:, None])
        .reshape(total_rows)
        .astype(jnp.float32)
    )
    row_prob = route_prob[0]
    gate_part = jnp.dot(token_rows, w_gate[0], preferred_element_type=jnp.float32)
    up_part = jnp.dot(token_rows, w_up[0], preferred_element_type=jnp.float32)
    down_part = jnp.dot(grad_rows, w_down[0], preferred_element_type=jnp.float32)
    gate_sum, up_sum, down_sum = lax.psum((gate_part, up_part, down_part), "fsdp")
    scaled_hidden, gate_act_grad, up_act_grad, prob_full = hidden_backward(
        gate_sum, up_sum, down_sum, row_prob, live_mask
    )
    share_rows = total_rows // lax.axis_size("fsdp")
    prob_grad = lax.dynamic_slice_in_dim(prob_full, lax.axis_index("fsdp") * share_rows, share_rows)
    over_rows = (((0,), (0,)), ((), ()))
    gate_grad = lax.dot_general(
        token_rows, gate_act_grad, over_rows, preferred_element_type=jnp.float32
    )
    up_grad = lax.dot_general(
        token_rows, up_act_grad, over_rows, preferred_element_type=jnp.float32
    )
    down_grad = lax.dot_general(
        grad_rows, scaled_hidden, over_rows, preferred_element_type=jnp.float32
    )
    over_hidden = (((1,), (1,)), ((), ()))
    slot_grad = (
        lax.dot_general(gate_act_grad, w_gate[0], over_hidden, preferred_element_type=jnp.float32)
        + lax.dot_general(up_act_grad, w_up[0], over_hidden, preferred_element_type=jnp.float32)
    ).astype(jnp.bfloat16)
    returned = lax.all_to_all(
        slot_grad.reshape(source_count, slot_count, feature_count),
        "expert",
        split_axis=0,
        concat_axis=0,
        tiled=True,
    )
    token_count = tokens.shape[0]
    route_table = (
        sent_rows.reshape(-1)[None, :] == jnp.arange(token_count, dtype=jnp.int32)[:, None]
    ).astype(jnp.bfloat16)
    token_grad = jnp.dot(
        route_table, returned.reshape(-1, feature_count), preferred_element_type=jnp.float32
    ).astype(jnp.bfloat16)
    return (token_grad, gate_grad[None], up_grad[None], down_grad[None], prob_grad[None])


def solution(mesh):
    return jax.shard_map(
        local,
        mesh=mesh,
        in_specs=(
            P("expert", "fsdp"),
            P("expert", "fsdp"),
            P("expert", None, None),
            P("expert", None),
            P("expert", None),
            P("expert", "fsdp", None),
            P("expert", "fsdp", None),
            P("expert", "fsdp", None),
        ),
        out_specs=(
            P("expert", "fsdp"),
            P("expert", "fsdp", None),
            P("expert", "fsdp", None),
            P("expert", "fsdp", None),
            P("expert", "fsdp"),
        ),
        check_vma=False,
    )
```

profile of v0, /device:TPU:1, one launch (start us, length us, event | category | flops | bytes accessed | tf_op | source)
XLA Modules:
  0.0 510.0 jit_solution(9055457515326459240)
XLA Ops:
  7.2 0.0 copy-start
  7.2 0.0 copy-start.2
  7.2 0.8 compare_select_fusion
  7.9 0.1 reshape.76
  8.0 1.1 copy.16
  9.1 1.4 gather_fusion.1
  10.5 7.5 %all-to-all-start.1 = ((bf16[8,24,80]{2,1,0:T(8,128)(2,1)}), bf16[8,24,80]{2,1,0:T(8,128)(2,1)S(1)}, u32[]{:S(2)}, u32[]{:S(2)}) async-start(bf16[8,24,80]{2,1,0:T(8,128)(2,1)} %bitcast.6), calls=%async_computation.1 | async-start | bytes 98304 | tf_op jit(solution)/shard_map/all_to_all | solution.py:25
  18.0 1.1 copy.15
  19.1 1.4 gather_fusion
  20.5 4.2 all-to-all-done.1
  24.7 3.3 all-to-all-start
  28.0 0.0 all-reduce.3.cloned.1.call-start
  28.1 0.0 copy-done.2
  28.1 0.0 copy-start.3
  28.1 1.3 fusion.12
  29.4 0.0 copy-done
  29.4 1.3 fusion.9
  30.7 3.9 all-to-all-done
  34.6 0.0 copy-done.3
  34.6 1.3 fusion.14
  35.9 0.0 copy-start.4
  35.9 0.0 copy-start.6
  36.0 0.0 copy-start.5
  36.0 0.0 all-reduce.3.cloned.1.call-update
  36.0 0.7 copy-done.4
  36.6 0.1 eq.15
  36.7 0.0 copy-done.6
  36.7 0.1 iota_compare_fusion.2
  36.8 0.1 lt.42
  36.9 0.0 copy-done.5
  36.9 444.8 %all-reduce.3.cloned.1.call-done = (f32[192,1536]{1,0:T(8,128)}, f32[192,1536]{1,0:T(8,128)}, f32[192,1536]{1,0:T(8,128)}) async-done(((f32[192,1536]{1,0:T(8,128)}, f32[192,1536]{1,0:T(8,128)}, f32[192,1536]{1,0:T(8,128)}), (f32[192,1536]{1,0:T(8,128)}, f32[192,1536]{1,0:T(8,128)}, f32[192,1536]{1,0:T(8,128)})) %all-reduce.3.cloned.1.call-update) | async-done | bytes 3538960 | tf_op jit(solution)/shard_map/psum | solution.py:41
  481.7 0.0 copy-start.1
  481.7 2.9 multiply_convert_fusion.1
  484.6 0.0 copy-done.1
  484.6 0.2 fusion.1
  484.8 1.1 convolution_bitcast_fusion
  485.9 0.3 fusion.7
  486.2 1.0 convolution_bitcast_fusion.2
  487.3 1.0 convolution_bitcast_fusion.1
  488.3 0.3 fusion.3
  488.6 0.7 copy.17
  489.3 6.1 %all-to-all-start.2 = ((bf16[8,24,80]{2,1,0:T(8,128)(2,1)}), bf16[8,24,80]{2,1,0:T(8,128)(2,1)S(1)}, u32[]{:S(2)}, u32[]{:S(2)}) async-start(bf16[8,24,80]{2,1,0:T(8,128)(2,1)} %bitcast.10), calls=%async_computation.2 | async-start | bytes 98304 | tf_op jit(solution)/shard_map/all_to_all | solution.py:62
  495.5 0.6 dynamic-slice_bitcast_fusion
  496.0 6.1 %all-to-all-done.2 = bf16[8,24,80]{2,1,0:T(8,128)(2,1)S(1)} async-done(((bf16[8,24,80]{2,1,0:T(8,128)(2,1)}), bf16[8,24,80]{2,1,0:T(8,128)(2,1)S(1)}, u32[]{:S(2)}, u32[]{:S(2)}) %all-to-all-start.2) | async-done | bytes 30752 | tf_op jit(solution)/shard_map/all_to_all | solution.py:62
  502.1 1.0 convolution_convert_fusion
  (3 shorter events, 0.0 us)
Async XLA Ops:
  7.2 22.3 %copy-start = (bf16[1,80,1536]{2,1,0:T(8,128)(2,1)S(1)}, bf16[1,80,1536]{2,1,0:T(8,128)(2,1)}, u32[]{:S(2)}) copy-start(bf16[1,80,1536]{2,1,0:T(8,128)(2,1)} %param.13) | copy-start | bytes 737284
  7.2 20.9 %copy-start.2 = (bf16[1,80,1536]{2,1,0:T(8,128)(2,1)S(1)}, bf16[1,80,1536]{2,1,0:T(8,128)(2,1)}, u32[]{:S(2)}) copy-start(bf16[1,80,1536]{2,1,0:T(8,128)(2,1)} %param.14) | copy-start | bytes 737284
  10.5 14.1 %all-to-all-start.1 = ((bf16[8,24,80]{2,1,0:T(8,128)(2,1)}), bf16[8,24,80]{2,1,0:T(8,128)(2,1)S(1)}, u32[]{:S(2)}, u32[]{:S(2)}) async-start(bf16[8,24,80]{2,1,0:T(8,128)(2,1)} %bitcast.6), calls=%async_computation.1 | async-start | bytes 98304 | tf_op jit(solution)/shard_map/all_to_all | solution.py:25
  24.7 9.9 %all-to-all-start = ((bf16[8,24,80]{2,1,0:T(8,128)(2,1)}), bf16[8,24,80]{2,1,0:T(8,128)(2,1)S(1)}, u32[]{:S(2)}, u32[]{:S(2)}) async-start(bf16[8,24,80]{2,1,0:T(8,128)(2,1)} %bitcast.1), calls=%async_computation | async-start | bytes 98304 | tf_op jit(solution)/shard_map/all_to_all | solution.py:26
  28.0 453.7 %all-reduce.3.cloned.1.call-start = ((), (), s32[]{:S(2)}) async-start(), calls=%async_computation.3 | async-start | bytes 7077888 | tf_op jit(solution)/shard_map/psum | solution.py:41
  28.1 6.5 %copy-start.3 = (bf16[1,80,1536]{2,1,0:T(8,128)(2,1)S(1)}, bf16[1,80,1536]{2,1,0:T(8,128)(2,1)}, u32[]{:S(2)}) copy-start(bf16[1,80,1536]{2,1,0:T(8,128)(2,1)} %param.15) | copy-start | bytes 737284
  35.9 0.7 copy-start.4
  35.9 0.8 copy-start.6
  36.0 0.9 copy-start.5
  481.7 2.9 copy-start.1
  489.3 12.8 %all-to-all-start.2 = ((bf16[8,24,80]{2,1,0:T(8,128)(2,1)}), bf16[8,24,80]{2,1,0:T(8,128)(2,1)S(1)}, u32[]{:S(2)}, u32[]{:S(2)}) async-start(bf16[8,24,80]{2,1,0:T(8,128)(2,1)} %bitcast.10), calls=%async_computation.2 | async-start | bytes 98304 | tf_op jit(solution)/shard_map/all_to_all | solution.py:62
Sparse Core Ops, SparseCore 0:
  36.1 445.5 all-reduce.2
where the time goes:
time: 514 us; the launch traced here: 510 us
  waiting for transfers between devices  459 us (89%)
  starting transfers between devices  17 us (3%)
  between operations  14.1 us (3%)
  matrix products  8.81 us (2%)
  local copies, waits for them, and re-layouts  7.22 us (1%)
    psum x1, waiting for transfers between devices, local(): lax.psum((gate_part, up_part, down_part), 'fsdp')  445 us
  transfers between devices with their start and end apart: 4, of which 4 were waited for; matrix products, arithmetic and copies ran while one was open for 1% of the time, Pallas kernels for 0%

commit v1 on v0

v1 whole, which is shorter than its diff:
```python
import functools

import jax
import jax.numpy as jnp
from jax import lax
from jax.experimental import pallas as pl
from jax.experimental.pallas import tpu as pltpu
from jax.sharding import PartitionSpec as P

MESH = pl.DeviceIdType.MESH
F32, BF16 = jnp.float32, jnp.bfloat16

Z = 16
EXP = 8
SLOT = 24
ROWS = EXP * SLOT
HALF = ROWS // 2
D_DEV = 80
KPAD = 128
FF = 1536
COLS = 384
NC = FF // COLS
TOK = 1024
NT = (((1,), (1,)), ((), ()))


def dot(a, b, dims=(((1,), (0,)), ((), ()))):
    return lax.dot_general(a, b, dims, preferred_element_type=F32)


def kernel(
    slots_ref, prob_ref, live_ref, tok_ref, grd_ref, wg_ref, wu_ref, wd_ref,
    tg_ref, gg_ref, ug_ref, dg_ref, pg_ref,
    onehot, sent, mine, other, weights, part, up_in, down_in, peer_out, peer_in, act, prob, prob_out, prob_in,
    back_out, back_in,
    mine_send, mine_recv, other_send, other_recv, w_send, w_recv,
    up_send, up_recv, down_send, down_recv, peer_send, peer_recv,
    ag_up_send, ag_down_send, ag_recv, pair_send, pair_recv,
    pr_up_send, pr_down_send, pr_recv, pp_send, pp_recv, back_send, back_recv,
):
    me = lax.axis_index("fsdp")
    ex = lax.axis_index("expert")
    core = lax.rem(me, 2)
    z = lax.rem(me // 2, Z)
    y = me // (2 * Z)
    d = 1 - 2 * core
    partner = me + d

    def at_z(pos):
        return (y * Z + pos) * 2 + core

    def wrap(pos):
        return lax.rem(pos + 2 * Z, Z)

    ahead, behind = at_z(wrap(z + d)), at_z(wrap(z - d))
    y_peer = ((1 - y) * Z + z) * 2 + core

    def remote(src, dst, send, recv, f, e):
        return pltpu.make_async_remote_copy(
            src_ref=src, dst_ref=dst, send_sem=send, recv_sem=recv,
            device_id={"fsdp": f, "expert": e}, device_id_type=MESH)

    barrier = pltpu.get_barrier_semaphore()
    for f in (partner, ahead, behind, y_peer):
        pl.semaphore_signal(barrier, inc=1, device_id={"fsdp": f, "expert": ex}, device_id_type=MESH)
    for k in range(1, EXP):
        e = lax.rem(ex + k, EXP)
        for f in (me, partner):
            pl.semaphore_signal(barrier, inc=1, device_id={"fsdp": f, "expert": e}, device_id_type=MESH)

    columns = lax.broadcasted_iota(jnp.int32, (ROWS, TOK), 1)
    onehot[...] = jnp.where(slots_ref[...] == columns, 1.0, 0.0).astype(BF16)
    for i, src in enumerate((tok_ref, grd_ref)):
        rows = dot(onehot[...], src[...], NT)
        rows = jnp.concatenate([rows, jnp.zeros((ROWS, KPAD - D_DEV), F32)], axis=1)
        sent[:, i] = rows.reshape(EXP, SLOT, KPAD).astype(BF16)
    pad = jnp.zeros((KPAD - D_DEV, FF), BF16)
    for i, w in enumerate((wg_ref, wu_ref, wd_ref)):
        weights[i, 0:D_DEV] = w[...]
        weights[i, D_DEV:KPAD] = pad
        weights[i, KPAD + D_DEV:2 * KPAD] = pad

    pl.semaphore_wait(barrier, 4 + 2 * (EXP - 1))

    def mine_copy(k):
        e = lax.rem(ex + k, EXP)
        return remote(sent.at[e], mine.at[ex], mine_send.at[e], mine_recv.at[ex], me, e)

    def other_copy(k):
        e = lax.rem(ex + k, EXP)
        return remote(sent.at[e], other.at[ex], other_send.at[e], other_recv.at[ex], partner, e)

    def mine_in(k):
        e = lax.rem(ex + k, EXP)
        return remote(sent.at[e], mine.at[e], mine_send.at[e], mine_recv.at[e], me, e)

    def other_in(k):
        e = lax.rem(ex + k, EXP)
        return remote(sent.at[e], other.at[e], other_send.at[e], other_recv.at[e], partner, e)

    def w_copy(i):
        src = (wg_ref, wu_ref, wd_ref)[i]
        return remote(src, weights.at[i, pl.ds(KPAD, D_DEV)], w_send.at[i], w_recv.at[i], partner, ex)

    for k in range(EXP):
        other_copy(k).start()
    for k in range(1, EXP):
        mine_copy(k).start()
    for i in range(3):
        w_copy(i).start()
    mine[ex] = sent[ex]
    for i in range(3):
        w_copy(i).wait_recv()
    for k in range(EXP):
        other_in(k).wait_recv()
    for k in range(1, EXP):
        mine_in(k).wait_recv()

    own_rows = [
        jnp.concatenate([
            mine[pl.ds(4 * core, 4), i].astype(F32).reshape(HALF, KPAD),
            other[pl.ds(4 * core, 4), i].astype(F32).reshape(HALF, KPAD),
        ], axis=1).astype(BF16)
        for i in range(2)
    ]
    for c in range(NC):
        for i in range(3):
            out = dot(own_rows[i // 2], weights[i, :, c * COLS:(c + 1) * COLS])
            for r in range(4):
                part[r * NC + c, i] = out[r * SLOT:(r + 1) * SLOT]

    def up_copy(s, i, src):
        return remote(src, up_in.at[s, i], up_send.at[s, i], up_recv.at[s, i], ahead, ex)

    def down_copy(s, i, src):
        return remote(src, down_in.at[s, i], down_send.at[s, i], down_recv.at[s, i], behind, ex)

    for i in range(3):
        up_copy(0, i, part.at[wrap(z + 8 * d), i]).start()
        down_copy(0, i, part.at[wrap(z - 7 * d), i]).start()

    def up_step(s, i):
        up_copy(s - 1, i, up_in.at[s - 1, i]).wait_recv()
        up_in[s - 1, i] = up_in[s - 1, i] + part[wrap(z + d * (8 - s)), i]
        up_copy(s, i, up_in.at[s - 1, i]).start()

    def down_step(s, i):
        down_copy(s - 1, i, down_in.at[s - 1, i]).wait_recv()
        down_in[s - 1, i] = down_in[s - 1, i] + part[wrap(z - d * (7 - s)), i]
        down_copy(s, i, down_in.at[s - 1, i]).start()

    def ring_step(s, _):
        for i in range(3):
            up_step(s, i)
            down_step(s, i)
        return 0

    lax.fori_loop(1, 7, ring_step, 0)
    for i in range(3):
        up_step(7, i)

    def peer_copy(i):
        return remote(peer_out.at[i], peer_in.at[i], peer_send.at[i], peer_recv.at[i], y_peer, ex)

    for i in range(3):
        down_copy(6, i, down_in.at[6, i]).wait_recv()
        up_copy(7, i, up_in.at[7, i]).wait_recv()
        peer_out[i] = (up_in[7, i] + down_in[6, i]) + part[z, i]
        peer_copy(i).start()
    for i in range(3):
        peer_copy(i).wait_recv()
    gate, up, down = (peer_out[i] + peer_in[i] for i in range(3))

    source = 4 * core + z // NC
    live = live_ref[source]
    scale = prob_ref[source] * live
    sigmoid = jax.nn.sigmoid(gate)
    silu = gate * sigmoid
    hidden = (silu * up).astype(BF16).astype(F32)
    hidden_grad = down * scale
    act[core, z, 0] = (hidden_grad * up * sigmoid * (1.0 + gate * (1.0 - sigmoid))).astype(BF16)
    act[core, z, 1] = (hidden_grad * silu).astype(BF16)
    act[core, z, 2] = (hidden * scale).astype(BF16)
    prob[z] = jnp.broadcast_to(live * jnp.sum(hidden * down, axis=1, keepdims=True), (SLOT, 128))

    def ag_up(s, i):
        owner = wrap(z - d * s)
        return remote(act.at[core, owner, i], act.at[core, owner, i], ag_up_send.at[s, i], ag_recv.at[owner, i], ahead, ex)

    def ag_down(s, i):
        owner = wrap(z + d * s)
        return remote(act.at[core, owner, i], act.at[core, owner, i], ag_down_send.at[s, i], ag_recv.at[owner, i], behind, ex)

    def pair_copy(half, owner, i):
        return remote(act.at[half, owner, i], act.at[half, owner, i], pair_send.at[owner, i], pair_recv.at[owner, i], partner, ex)

    def pr_up(s):
        owner = wrap(z - d * s)
        return remote(prob.at[owner], prob.at[owner], pr_up_send.at[s], pr_recv.at[owner], ahead, ex)

    def pr_down(s):
        owner = wrap(z + d * s)
        return remote(prob.at[owner], prob.at[owner], pr_down_send.at[s], pr_recv.at[owner], behind, ex)

    for i in range(3):
        ag_up(0, i).start()
        ag_down(0, i).start()
    pr_up(0).start()
    pr_down(0).start()
    for i in range(3):
        pair_copy(core, z, i).start()

    def gather_step(s, _):
        for i in range(3):
            ag_up(s, i).wait_recv()
            ag_up(s, i).start()
            ag_down(s, i).wait_recv()

            @pl.when(s < 7)
            def _():
                ag_down(s, i).start()

        for i in range(3):
            pair_copy(core, wrap(z - d * s), i).start()
            pair_copy(core, wrap(z + d * s), i).start()

        @pl.when(s < 4)
        def _():
            pr_up(s).wait_recv()
            pr_down(s).wait_recv()

            @pl.when(s < 3)
            def _():
                pr_up(s).start()
                pr_down(s).start()

        return 0

    lax.fori_loop(1, 8, gather_step, 0)
    for i in range(3):
        ag_up(8, i).wait_recv()
        pair_copy(core, wrap(z + 8), i).start()

    group = z // NC
    prob_out[...] = sum(prob[group * NC + c] for c in range(NC))
    pp = remote(prob_out, prob_in, pp_send, pp_recv, partner, ex)
    pp.start()

    def pair_wait(owner, _):
        for i in range(3):
            pair_copy(1 - core, owner, i).wait_recv()
        return 0

    lax.fori_loop(0, Z, pair_wait, 0)

    def full(i, c):
        return jnp.concatenate(
            [act[h, r * NC + c, i].astype(F32) for h in range(2) for r in range(4)], axis=0).astype(BF16)

    acts = [[full(i, c) for c in range(NC)] for i in range(3)]
    slot_grad = jnp.zeros((ROWS, D_DEV), F32)
    for c in range(NC):
        cols = slice(c * COLS, (c + 1) * COLS)
        slot_grad += dot(acts[0][c], wg_ref[:, cols], NT)
        slot_grad += dot(acts[1][c], wu_ref[:, cols], NT)
    slot_grad = jnp.concatenate([slot_grad, jnp.zeros((ROWS, KPAD - D_DEV), F32)], axis=1)
    back_out[...] = slot_grad.reshape(EXP, SLOT, KPAD).astype(BF16)

    def back_copy(k):
        e = lax.rem(ex + k, EXP)
        return remote(back_out.at[e], back_in.at[ex], back_send.at[e], back_recv.at[ex], me, e)

    def back_wait(k):
        e = lax.rem(ex + k, EXP)
        return remote(back_out.at[e], back_in.at[e], back_send.at[e], back_recv.at[e], me, e)

    for k in range(1, EXP):
        back_copy(k).start()
    back_in[ex] = back_out[ex]

    rows_t = [mine[:, i].astype(F32).reshape(ROWS, KPAD).T.astype(BF16) for i in range(2)]
    for i, out in enumerate((gg_ref, ug_ref, dg_ref)):
        for c in range(NC):
            out[:, c * COLS:(c + 1) * COLS] = dot(rows_t[i // 2], acts[i][c])[:D_DEV]

    pp.wait()
    total = jnp.where(core == y, prob_out[...], prob_in[...])
    first = 3 * (lax.rem(z, NC) * 2 + core)
    row = lax.broadcasted_iota(jnp.int32, (SLOT, 128), 0)
    lane = lax.broadcasted_iota(jnp.int32, (SLOT, 128), 1)
    picked = jnp.sum(jnp.where(row == first + lane, total, 0.0), axis=0, keepdims=True)
    pg_ref[...] = picked[:, :3]

    for k in range(1, EXP):
        back_wait(k).wait_recv()
    back_t = back_in[...].astype(F32).reshape(ROWS, KPAD).T.astype(BF16)
    tg_ref[...] = dot(back_t, onehot[...])[:D_DEV].astype(BF16)

    for k in range(EXP):
        other_copy(k).wait_send()
    for k in range(1, EXP):
        mine_copy(k).wait_send()
        back_copy(k).wait_send()
    for i in range(3):
        w_copy(i).wait_send()
        peer_copy(i).wait_send()
    for s in range(3):
        pr_up(s).wait_send()
        pr_down(s).wait_send()

    def drain(s, _):
        for i in range(3):
            up_copy(s, i, up_in.at[s, i]).wait_send()
            ag_up(s, i).wait_send()

            @pl.when(s < 7)
            def _():
                down_copy(s, i, down_in.at[s, i]).wait_send()
                ag_down(s, i).wait_send()

        return 0

    lax.fori_loop(0, 8, drain, 0)

    def pair_drain(owner, _):
        for i in range(3):
            pair_copy(core, owner, i).wait_send()
        return 0

    lax.fori_loop(0, Z, pair_drain, 0)


def local(tokens, out_grad, slot_rows, expert_counts, route_prob, w_gate, w_up, w_down):
    slots = slot_rows[0].reshape(ROWS, 1)
    live = (jnp.arange(SLOT, dtype=jnp.int32)[None, :] < expert_counts[0][:, None]).astype(F32)[:, :, None]
    prob = route_prob[0].reshape(EXP, SLOT, 1)
    vmem = pl.BlockSpec(memory_space=pltpu.VMEM)
    dma = pltpu.SemaphoreType.DMA
    grad = jax.ShapeDtypeStruct((D_DEV, FF), F32)
    tg, gg, ug, dg, pg = pl.pallas_call(
        kernel,
        out_shape=(jax.ShapeDtypeStruct((D_DEV, TOK), BF16), grad, grad, grad, jax.ShapeDtypeStruct((1, 3), F32)),
        in_specs=[vmem] * 8,
        out_specs=(vmem,) * 5,
        scratch_shapes=[
            pltpu.VMEM((ROWS, TOK), BF16),
            pltpu.VMEM((EXP, 2, SLOT, KPAD), BF16),
            pltpu.VMEM((EXP, 2, SLOT, KPAD), BF16),
            pltpu.VMEM((EXP, 2, SLOT, KPAD), BF16),
            pltpu.VMEM((3, 2 * KPAD, FF), BF16),
            pltpu.VMEM((Z, 3, SLOT, COLS), F32),
            pltpu.VMEM((8, 3, SLOT, COLS), F32),
            pltpu.VMEM((7, 3, SLOT, COLS), F32),
            pltpu.VMEM((3, SLOT, COLS), F32),
            pltpu.VMEM((3, SLOT, COLS), F32),
            pltpu.VMEM((2, Z, 3, SLOT, COLS), BF16),
            pltpu.VMEM((Z, SLOT, 128), F32),
            pltpu.VMEM((SLOT, 128), F32),
            pltpu.VMEM((SLOT, 128), F32),
            pltpu.VMEM((EXP, SLOT, KPAD), BF16),
            pltpu.VMEM((EXP, SLOT, KPAD), BF16),
            dma((EXP,)), dma((EXP,)), dma((EXP,)), dma((EXP,)), dma((3,)), dma((3,)),
            dma((8, 3)), dma((8, 3)), dma((7, 3)), dma((7, 3)), dma((3,)), dma((3,)),
            dma((8, 3)), dma((7, 3)), dma((Z, 3)), dma((Z, 3)), dma((Z, 3)),
            dma((3,)), dma((3,)), dma((Z,)), dma, dma, dma((EXP,)), dma((EXP,)),
        ],
        compiler_params=pltpu.CompilerParams(collective_id=0, has_side_effects=True),
    )(slots, prob, live, tokens.T, out_grad.T, w_gate[0], w_up[0], w_down[0])
    return tg.T, gg[None], ug[None], dg[None], pg


def solution(mesh):
    return jax.shard_map(
        local,
        mesh=mesh,
        in_specs=(
            P("expert", "fsdp"),
            P("expert", "fsdp"),
            P("expert", None, None),
            P("expert", None),
            P("expert", None),
            P("expert", "fsdp", None),
            P("expert", "fsdp", None),
            P("expert", "fsdp", None),
        ),
        out_specs=(
            P("expert", "fsdp"),
            P("expert", "fsdp", None),
            P("expert", "fsdp", None),
            P("expert", "fsdp", None),
            P("expert", "fsdp"),
        ),
        check_vma=False,
    )
```

time: 514 us -> 101 us (0.20)
  waiting for transfers between devices: 459 us -> 0 us
  Pallas kernels: 0 us -> 90.8 us
  starting transfers between devices: 17 us -> 0 us
  between operations: 14.1 us -> 0.67 us
  matrix products: 8.81 us -> 0 us
    psum x1 -> x0, waiting for transfers between devices: 445 us -> none  [local(): lax.psum((gate_part, up_part, down_part), 'fsdp')]
    pallas_call x0 -> x1, Pallas kernels: none -> 90.8 us  [local(): pl.pallas_call(kernel, out_shape=(jax.ShapeDtypeStruct((D_DEV, TOK), BF16...]
    all_to_all x3 -> x0, starting transfers between devices: 16.9 us -> none  [the longest x1 7.47 us: local(): lax.all_to_all(tokens[sent_rows], 'expert', split_axis=0, concat_axis=0,...]
    all_to_all x3 -> x0, waiting for transfers between devices: 14.1 us -> none  [the longest x1 6.06 us: local(): lax.all_to_all(slot_grad.reshape(source_count, slot_count, feature_count)...]
    dot_general x9 -> x0, matrix products: 8.81 us -> none  [the longest x1 1.35 us: local(): up_part = jnp.dot(token_rows, w_up[0], preferred_element_type=jnp.float32)]
  transfers between devices with their start and end apart: 4 -> 0, of which waited for: 4 -> 0; matrix products, arithmetic and copies ran while one was open for 1% -> 0% of each run, Pallas kernels for 0% -> 0%
where the time goes in v1:
time: 101 us
  Pallas kernels  90.8 us (90%)
  local copies, waits for them, and re-layouts  8.26 us (8%)
  other arithmetic  1.38 us (1%)
    pallas_call x1, Pallas kernels, local(): pl.pallas_call(kernel, out_shape=(jax.ShapeDtypeStruct((D_DEV, TOK), BF16...  90.8 us
    unnamed x18, local copies, waits for them, and re-layouts  6.68 us

profile of v1, /device:TPU:1, one launch (start us, length us, event | category | flops | bytes accessed | tf_op | source)
XLA Modules:
  0.0 101.1 jit_solution(5933247070644453945)
XLA Ops:
  0.6 0.0 copy-start.3
  0.6 0.5 broadcast.24
  1.2 0.2 copy-done.3
  1.3 0.7 reduce.3
  2.0 0.0 copy-start.2
  2.0 0.8 reshape_squeeze.9.prob_ref
  2.8 0.0 copy-done.2
  2.8 0.0 copy-start.4
  2.8 0.7 reshape_squeeze.8.slots_ref
  3.6 0.0 copy-done.4
  3.6 0.7 fusion.live_ref
  4.3 90.8 %shard_map.119 = (bf16[80,1024]{1,0:T(8,128)(2,1)}, f32[80,1536]{1,0:T(8,128)}, f32[80,1536]{1,0:T(8,128)}, f32[80,1536]{1,0:T(8,128)}, f32[1,3]{1,0:T(1,128)}) custom-call(s32[192,1]{1,0:T(8,128)} %reshape_squeeze.8.slots_ref, f32[8,24,1]{2,1,0:T(8,128)} %reshape_squeeze.9.prob_ref, f32[8,24,1]{2,1,0:T(8,128)} %fusion.live_ref, bf16[80,1024]{1,0:T(8,128)(2,1)} %bitcast.17, ...), custom_call_target="tpu_custom_call" | custom-call | tf_op jit(solution)/shard_map/pallas_call | solution.py:340
  95.1 1.6 %copy.20 = bf16[1024,80]{0,1:T(8,128)(2,1)} copy(bf16[1024,80]{0,1:T(8,128)(2,1)} %bitcast.16) | data formatting | bytes 327680
  96.7 0.0 copy-start.1
  96.7 1.9 %copy.21 = f32[1,80,1536]{2,1,0:T(8,128)} copy(f32[1,80,1536]{2,1,0:T(8,128)} %bitcast.12) | data formatting | bytes 983040
  98.6 0.0 copy-done.1
  98.6 0.0 copy-start
  98.6 0.8 copy.22
  99.4 0.4 copy-done
  99.8 0.0 copy-start.5
  99.8 0.8 copy.23
  100.6 0.0 copy-done.5
  100.6 0.5 copy.24
Async XLA Ops:
  0.6 0.7 copy-start.3
  2.0 0.9 copy-start.2
  2.8 0.7 copy-start.4
  96.7 1.9 %copy-start.1 = (f32[80,1536]{1,0:T(8,128)S(1)}, f32[80,1536]{1,0:T(8,128)}, u32[]{:S(2)}) copy-start(f32[80,1536]{1,0:T(8,128)} %get-tuple-element.12) | copy-start | bytes 1474564
  98.6 1.2 %copy-start = (f32[80,1536]{1,0:T(8,128)S(1)}, f32[80,1536]{1,0:T(8,128)}, u32[]{:S(2)}) copy-start(f32[80,1536]{1,0:T(8,128)} %get-tuple-element.13) | copy-start | bytes 1474564
  99.8 0.8 copy-start.5

commit v2 on v0

v2 whole, which is shorter than its diff:
```python
import jax
import jax.numpy as jnp
from jax import lax
from jax.experimental import pallas as pl
from jax.experimental.pallas import tpu as pltpu
from jax.sharding import PartitionSpec as P

MESH = pl.DeviceIdType.MESH
F32, BF16 = jnp.float32, jnp.bfloat16

Z = 16
EXP = 8
SLOT = 24
ROWS = EXP * SLOT
HALF = ROWS // 2
D_DEV = 80
KPAD = 128
FF = 1536
COLS = 384
NC = FF // COLS
TOK = 1024
SUB = 1
NB = 4
NT = (((1,), (1,)), ((), ()))


def dot(a, b, dims=(((1,), (0,)), ((), ()))):
    return lax.dot_general(a, b, dims, preferred_element_type=F32)


def slot_column(slots_ref):
    wide = jnp.concatenate([slots_ref[0].astype(F32), jnp.zeros((EXP, KPAD - SLOT), F32)], axis=1)
    tall = wide.T
    return jnp.concatenate([tall[:SLOT, e:e + 1] for e in range(EXP)], axis=0)


def one_hot(slots_ref, first, width):
    columns = lax.broadcasted_iota(jnp.int32, (ROWS, width), 1) + first
    return jnp.where(slot_column(slots_ref) == columns.astype(F32), 1.0, 0.0).astype(BF16)


def pad_features(rows):
    return jnp.concatenate([rows, jnp.zeros((ROWS, KPAD - D_DEV), F32)], axis=1)


def kernel(
    slots_ref, prob_ref, counts_ref, tok_ref, grd_ref, wg_ref, wu_ref, wd_ref,
    acts_ref, rows_ref, back_ref, pg_ref,
    sent, mine, other, weights, part, up_in, down_in, fin_in, own_in, act, acts, rows_t,
    prob, prob_out, prob_in, back_out, back_in,
    mine_send, mine_recv, other_send, other_recv, w_send, w_recv,
    up_send, up_recv, down_send, down_recv, fin_send, fin_recv, own_send, own_recv,
    ag_send, ag_recv, pair_send, pair_recv, pr_send, pr_recv, pp_send, pp_recv, back_send, back_recv, out_sem,
):
    me = lax.axis_index("fsdp")
    ex = lax.axis_index("expert")
    core = lax.rem(me, 2)
    z = lax.rem(me // 2, Z)
    y = me // (2 * Z)
    d = 1 - 2 * core
    partner = me + d

    def at_z(pos, plane=None):
        return ((y if plane is None else plane) * Z + pos) * 2 + core

    def wrap(pos):
        return lax.rem(pos + 2 * Z, Z)

    near = [at_z(wrap(z + d)), at_z(wrap(z - d))]
    far = [at_z(wrap(z + 2 * d)), at_z(wrap(z - 2 * d))]
    cross = [at_z(wrap(z + d), 1 - y), at_z(wrap(z - d), 1 - y)]
    y_peer = at_z(z, 1 - y)
    sign = (d, -d)
    pending = []

    def remote(src, dst, send, recv, f, e=None):
        return pltpu.make_async_remote_copy(
            src_ref=src, dst_ref=dst, send_sem=send, recv_sem=recv,
            device_id={"fsdp": f, "expert": ex if e is None else e}, device_id_type=MESH)

    def go(copy):
        copy.start()
        pending.append(copy)

    barrier = pltpu.get_barrier_semaphore()
    friends = [partner, y_peer] + near + far + cross
    for k in range(1, EXP):
        e = lax.rem(ex + k, EXP)
        for f in (me, partner):
            pl.semaphore_signal(barrier, inc=1, device_id={"fsdp": f, "expert": e}, device_id_type=MESH)
    for f in friends:
        pl.semaphore_signal(barrier, inc=1, device_id={"fsdp": f, "expert": ex}, device_id_type=MESH)

    table = one_hot(slots_ref, 0, TOK)
    for i, src in enumerate((tok_ref, grd_ref)):
        sent[:, i] = pad_features(dot(table, src[...], NT)).reshape(EXP, SLOT, KPAD).astype(BF16)
    pad = jnp.zeros((KPAD - D_DEV, FF), BF16)
    for i, w in enumerate((wg_ref, wu_ref, wd_ref)):
        weights[i, 0:D_DEV] = w[...]
        weights[i, D_DEV:KPAD] = pad
        weights[i, KPAD + D_DEV:2 * KPAD] = pad

    pl.semaphore_wait(barrier, len(friends) + 2 * (EXP - 1))

    def peer_expert(k):
        return lax.rem(ex + k, EXP)

    for k in range(EXP):
        e = peer_expert(k)
        go(remote(sent.at[e], other.at[ex], other_send.at[e], other_recv.at[ex], partner, e))
        if k:
            go(remote(sent.at[e], mine.at[ex], mine_send.at[e], mine_recv.at[ex], me, e))
    w_copies = [
        remote(w, weights.at[i, pl.ds(KPAD, D_DEV)], w_send.at[i], w_recv.at[i], partner)
        for i, w in enumerate((wg_ref, wu_ref, wd_ref))]
    for copy in w_copies:
        go(copy)
    mine[ex] = sent[ex]
    for copy in w_copies:
        copy.wait_recv()
    for k in range(EXP):
        e = peer_expert(k)
        remote(sent.at[e], other.at[e], other_send.at[e], other_recv.at[e], partner, e).wait_recv()
        if k:
            remote(sent.at[e], mine.at[e], mine_send.at[e], mine_recv.at[e], me, e).wait_recv()

    own_rows = [
        jnp.concatenate([
            mine[pl.ds(4 * core, 4), i].astype(F32).reshape(HALF, KPAD),
            other[pl.ds(4 * core, 4), i].astype(F32).reshape(HALF, KPAD),
        ], axis=1).astype(BF16)
        for i in range(2)
    ]
    for c in range(NC):
        for i in range(3):
            out = dot(own_rows[i // 2], weights[i, :, c * COLS:(c + 1) * COLS])
            for r in range(4):
                for g in range(3):
                    part[r * NC + c, g * 3 + i] = out[r * SLOT + g * 8:r * SLOT + g * 8 + 8]

    subs = [(q, pl.ds(q, SUB)) for q in range(0, 9, SUB)]

    def up_copy(a, q, block, src, skip=False):
        return remote(src, up_in.at[a - 1, block], up_send.at[a - 1, q], up_recv.at[a - 1, q], far[0] if skip else near[0])

    def down_copy(a, q, block, src):
        return remote(src, down_in.at[a - 1, block], down_send.at[a - 1, q], down_recv.at[a - 1, q], near[1])

    def fin_copy(way, other_plane, q, block, src):
        f = (cross if other_plane else near)[way]
        return remote(src, fin_in.at[way, other_plane, block], fin_send.at[way, other_plane, q],
                      fin_recv.at[way, other_plane, q], f)

    def own_copy(q, block):
        return remote(part.at[z, block], own_in.at[block], own_send.at[q], own_recv.at[q], y_peer)

    for q, block in subs:
        up_copy(8, q, block, part.at[wrap(z + 8 * d), block], True).start()
        up_copy(7, q, block, part.at[wrap(z + 7 * d), block]).start()
        down_copy(7, q, block, part.at[wrap(z - 7 * d), block]).start()
    for q, block in subs:
        own_copy(q, block).start()

    for i in range(2):
        rows_t[i] = mine[:, i].astype(F32).reshape(ROWS, KPAD).T.astype(BF16)
    rows_out = pltpu.make_async_copy(rows_t, rows_ref, out_sem.at[0])
    rows_out.start()

    def up_add(j, q, block):
        up_copy(j + 1, q, block, up_in.at[j, block]).wait_recv()
        up_in[j, block] = up_in[j, block] + part[wrap(z + d * j), block]

    def down_add(j, q, block):
        down_copy(j + 1, q, block, down_in.at[j, block]).wait_recv()
        down_in[j, block] = down_in[j, block] + part[wrap(z - d * j), block]

    for q, block in subs:
        down_add(6, q, block)
        down_copy(6, q, block, down_in.at[6, block]).start()
        up_copy(8, q, block, up_in.at[7, block], True).wait_recv()
        up_add(6, q, block)
        up_in[6, block] = up_in[6, block] + up_in[7, block]
        up_copy(6, q, block, up_in.at[6, block]).start()

    def ring_step(t, _):
        j = 5 - t
        for q, block in subs:
            down_add(j, q, block)
            down_copy(j, q, block, down_in.at[j, block]).start()
            up_add(j, q, block)
            up_copy(j, q, block, up_in.at[j, block]).start()
        return 0

    lax.fori_loop(0, 4, ring_step, 0)
    for q, block in subs:
        down_add(1, q, block)
        for other_plane in (1, 0):
            fin_copy(1, other_plane, q, block, down_in.at[1, block]).start()
        up_add(1, q, block)
        for other_plane in (1, 0):
            fin_copy(0, other_plane, q, block, up_in.at[1, block]).start()

    source = 4 * core + z // NC
    k8 = lax.broadcasted_iota(jnp.int32, (8, 1), 0)
    lane = lax.broadcasted_iota(jnp.int32, (8, ROWS), 1)
    count = jnp.sum(jnp.where(lax.broadcasted_iota(jnp.int32, (1, EXP), 1) == source, counts_ref[...].astype(F32), 0.0),
                    axis=1, keepdims=True)
    spot = lax.broadcasted_iota(jnp.int32, (8, 128), 1)

    def ag_copy(way, a, g, two):
        owner = wrap(z - sign[way] * a)
        return remote(act.at[core, owner, g], act.at[core, owner, g], ag_send.at[way, a + (2 if two else 1) - 1, g],
                      ag_recv.at[owner, g], (far if two else near)[way])

    def ag_arrival(way, a, g):
        owner = wrap(z - sign[way] * a)
        return remote(act.at[core, owner, g], act.at[core, owner, g], ag_send.at[way, 0, g], ag_recv.at[owner, g], near[way])

    def pair_copy(half, owner, g):
        return remote(act.at[half, owner, g], act.at[half, owner, g], pair_send.at[owner, g], pair_recv.at[owner, g], partner)

    def pr_copy(way, a, two):
        owner = wrap(z - sign[way] * a)
        return remote(prob.at[owner], prob.at[owner], pr_send.at[way, a + (2 if two else 1) - 1], pr_recv.at[owner],
                      (far if two else near)[way])

    last = (8, 7)

    def hand_on(a, g):
        for two in (True, False):
            for way in range(2):
                if a + (2 if two else 1) <= last[way]:
                    go(ag_copy(way, a, g, two))

    tile = jnp.zeros((8, 128), F32)
    for g in range(3):
        sums = []
        for i in range(3):
            q = (g * 3 + i) // SUB * SUB
            block = pl.ds(q, SUB)
            if (g * 3 + i) % SUB == 0:
                own_copy(q, block).wait_recv()
                for way in range(2):
                    for other_plane in range(2):
                        fin_copy(way, other_plane, q, block, fin_in.at[way, other_plane, block]).wait_recv()
            n = g * 3 + i
            here = (fin_in[0, 0, n] + fin_in[1, 0, n]) + part[z, n]
            there = (fin_in[0, 1, n] + fin_in[1, 1, n]) + own_in[n]
            sums.append(here + there)
        gate, up, down = sums
        slot = k8 + 8 * g
        live = (slot.astype(F32) < count).astype(F32)
        scale = live * jnp.sum(jnp.where(lane == slot + SLOT * source, prob_ref[...], 0.0), axis=1, keepdims=True)
        sigmoid = jax.nn.sigmoid(gate)
        silu = gate * sigmoid
        hidden = (silu * up).astype(BF16).astype(F32)
        hidden_grad = down * scale
        act[core, z, g, 0] = (hidden_grad * up * sigmoid * (1.0 + gate * (1.0 - sigmoid))).astype(BF16)
        act[core, z, g, 1] = (hidden_grad * silu).astype(BF16)
        act[core, z, g, 2] = (hidden * scale).astype(BF16)
        hand_on(0, g)
        go(pair_copy(core, z, g))
        tile += jnp.where(spot == g, live * jnp.sum(hidden * down, axis=1, keepdims=True), 0.0)
    prob[z] = tile
    for way in range(2):
        for two in (True, False):
            go(pr_copy(way, 0, two))

    for t in range(1, 5):
        for g in range(3):
            for way in range(2):
                if 2 * t <= last[way]:
                    ag_arrival(way, 2 * t, g).wait_recv()
            hand_on(2 * t, g)
            for way in range(2):
                if 2 * t <= last[way]:
                    go(pair_copy(core, wrap(z - sign[way] * 2 * t), g))
        for g in range(3):
            for way in range(2):
                ag_arrival(way, 2 * t - 1, g).wait_recv()
                go(pair_copy(core, wrap(z - sign[way] * (2 * t - 1)), g))
        if t == 1:
            for way in range(2):
                pr_copy(way, 2, False).wait_recv()
                go(pr_copy(way, 2, False))
                pr_copy(way, 1, False).wait_recv()
        if t == 2:
            for way in range(2):
                pr_copy(way, 3, False).wait_recv()
            group = z // NC
            prob_out[...] = sum(prob[group * NC + c] for c in range(NC))
            pp = remote(prob_out, prob_in, pp_send, pp_recv, partner)
            go(pp)

    def pair_wait(owner, _):
        for g in range(3):
            pair_copy(1 - core, owner, g).wait_recv()
        return 0

    lax.fori_loop(0, Z, pair_wait, 0)

    slot_grad = jnp.zeros((ROWS, D_DEV), F32)
    for c in range(NC):
        cols = slice(c * COLS, (c + 1) * COLS)
        for i in range(3):
            full = jnp.concatenate(
                [act[h, r * NC + c, g, i].astype(F32) for h in range(2) for r in range(4) for g in range(3)],
                axis=0).astype(BF16)
            acts[i, :, cols] = full
            if i < 2:
                slot_grad += dot(full, (wg_ref, wu_ref)[i][:, cols], NT)
    back_out[...] = pad_features(slot_grad).reshape(EXP, SLOT, KPAD).astype(BF16)
    for k in range(1, EXP):
        e = peer_expert(k)
        go(remote(back_out.at[e], back_in.at[ex], back_send.at[e], back_recv.at[ex], me, e))
    acts_out = pltpu.make_async_copy(acts, acts_ref, out_sem.at[1])
    acts_out.start()
    back_in[ex] = back_out[ex]

    pp.wait_recv()
    total = jnp.where(core == y, prob_out[...], prob_in[...])
    place = lax.broadcasted_iota(jnp.int32, (8, 128), 0) + 8 * spot
    first = 3 * (lax.rem(z, NC) * 2 + core)
    picked = [jnp.sum(jnp.where(place == first + j, total, 0.0), axis=(0, 1), keepdims=True) for j in range(3)]
    pg_ref[...] = jnp.concatenate(picked, axis=1)

    for copy in pending:
        copy.wait_send()

    def drain(a, _):
        for q, block in subs:
            up_copy(a, q, block, up_in.at[a - 1, block]).wait_send()
            down_copy(a, q, block, down_in.at[a - 1, block]).wait_send()
        return 0

    lax.fori_loop(2, 8, drain, 0)
    for q, block in subs:
        up_copy(8, q, block, up_in.at[7, block], True).wait_send()
        own_copy(q, block).wait_send()
        for way in range(2):
            for other_plane in range(2):
                fin_copy(way, other_plane, q, block, fin_in.at[way, other_plane, block]).wait_send()
    for k in range(1, EXP):
        e = peer_expert(k)
        remote(back_out.at[e], back_in.at[e], back_send.at[e], back_recv.at[e], me, e).wait_recv()
    back_out_copy = pltpu.make_async_copy(back_in, back_ref, out_sem.at[2])
    back_out_copy.start()
    rows_out.wait()
    acts_out.wait()
    back_out_copy.wait()


def last_kernel(slots_ref, acts_ref, rows_ref, back_ref, tg_ref, gg_ref, ug_ref, dg_ref):
    for i, out in enumerate((gg_ref, ug_ref, dg_ref)):
        out[0] = dot(rows_ref[i // 2], acts_ref[i])[:D_DEV]
    back_t = back_ref[...].astype(F32).reshape(ROWS, KPAD).T.astype(BF16)
    width = TOK // NB
    table = one_hot(slots_ref, pl.program_id(0) * width, width)
    tg_ref[...] = dot(back_t, table)[:D_DEV].astype(BF16)


def local(tokens, out_grad, slot_rows, expert_counts, route_prob, w_gate, w_up, w_down):
    vmem = pl.BlockSpec(memory_space=pltpu.VMEM)
    hbm = pl.BlockSpec(memory_space=pl.ANY)
    dma = pltpu.SemaphoreType.DMA
    shape = jax.ShapeDtypeStruct
    acts, rows, back, pg = pl.pallas_call(
        kernel,
        out_shape=(shape((3, ROWS, FF), BF16), shape((2, KPAD, ROWS), BF16), shape((EXP, SLOT, KPAD), BF16), shape((1, 3), F32)),
        in_specs=[vmem] * 8,
        out_specs=(hbm, hbm, hbm, vmem),
        scratch_shapes=[
            pltpu.VMEM((EXP, 2, SLOT, KPAD), BF16),
            pltpu.VMEM((EXP, 2, SLOT, KPAD), BF16),
            pltpu.VMEM((EXP, 2, SLOT, KPAD), BF16),
            pltpu.VMEM((3, 2 * KPAD, FF), BF16),
            pltpu.VMEM((Z, 9, 8, COLS), F32),
            pltpu.VMEM((8, 9, 8, COLS), F32),
            pltpu.VMEM((7, 9, 8, COLS), F32),
            pltpu.VMEM((2, 2, 9, 8, COLS), F32),
            pltpu.VMEM((9, 8, COLS), F32),
            pltpu.VMEM((2, Z, 3, 3, 8, COLS), BF16),
            pltpu.VMEM((3, ROWS, FF), BF16),
            pltpu.VMEM((2, KPAD, ROWS), BF16),
            pltpu.VMEM((Z, 8, 128), F32),
            pltpu.VMEM((8, 128), F32),
            pltpu.VMEM((8, 128), F32),
            pltpu.VMEM((EXP, SLOT, KPAD), BF16),
            pltpu.VMEM((EXP, SLOT, KPAD), BF16),
            dma((EXP,)), dma((EXP,)), dma((EXP,)), dma((EXP,)), dma((3,)), dma((3,)),
            dma((8, 9)), dma((8, 9)), dma((7, 9)), dma((7, 9)), dma((2, 2, 9)), dma((2, 2, 9)), dma((9,)), dma((9,)),
            dma((2, 8, 3)), dma((Z, 3)), dma((Z, 3)), dma((Z, 3)), dma((2, 3)), dma((Z,)), dma, dma,
            dma((EXP,)), dma((EXP,)), dma((3,)),
        ],
        compiler_params=pltpu.CompilerParams(collective_id=0, has_side_effects=True),
    )(slot_rows, route_prob, expert_counts, tokens.T, out_grad.T, w_gate[0], w_up[0], w_down[0])
    grad = shape((1, D_DEV, FF), F32)
    grad_spec = pl.BlockSpec((1, D_DEV, FF // NB), lambda n: (0, 0, n))
    tg, gg, ug, dg = pl.pallas_call(
        last_kernel,
        grid=(NB,),
        out_shape=(shape((D_DEV, TOK), BF16), grad, grad, grad),
        in_specs=[
            pl.BlockSpec((1, EXP, SLOT), lambda n: (0, 0, 0)),
            pl.BlockSpec((3, ROWS, FF // NB), lambda n: (0, 0, n)),
            pl.BlockSpec((2, KPAD, ROWS), lambda n: (0, 0, 0)),
            pl.BlockSpec((EXP, SLOT, KPAD), lambda n: (0, 0, 0)),
        ],
        out_specs=(pl.BlockSpec((D_DEV, TOK // NB), lambda n: (0, n)), grad_spec, grad_spec, grad_spec),
    )(slot_rows, acts, rows, back)
    return tg.T, gg, ug, dg, pg


def solution(mesh):
    return jax.shard_map(
        local,
        mesh=mesh,
        in_specs=(
            P("expert", "fsdp"),
            P("expert", "fsdp"),
            P("expert", None, None),
            P("expert", None),
            P("expert", None),
            P("expert", "fsdp", None),
            P("expert", "fsdp", None),
            P("expert", "fsdp", None),
        ),
        out_specs=(
            P("expert", "fsdp"),
            P("expert", "fsdp", None),
            P("expert", "fsdp", None),
            P("expert", "fsdp", None),
            P("expert", "fsdp"),
        ),
        check_vma=False,
    )
```

time: 514 us -> 86.7 us (0.17)
  waiting for transfers between devices: 459 us -> 0 us
  Pallas kernels: 0 us -> 85.3 us
  starting transfers between devices: 17 us -> 0 us
  between operations: 14.1 us -> 0.65 us
  matrix products: 8.81 us -> 0 us
  local copies, waits for them, and re-layouts: 7.22 us -> 0.52 us
    psum x1 -> x0, waiting for transfers between devices: 445 us -> none  [local(): lax.psum((gate_part, up_part, down_part), 'fsdp')]
    pallas_call x0 -> x2, Pallas kernels: none -> 85.3 us  [the longest x1 81.1 us: local(): pl.pallas_call(kernel, out_shape=(shape((3, ROWS, FF), BF16), shape((2, K...]
    all_to_all x3 -> x0, starting transfers between devices: 16.9 us -> none  [the longest x1 7.47 us: local(): lax.all_to_all(tokens[sent_rows], 'expert', split_axis=0, concat_axis=0,...]
    all_to_all x3 -> x0, waiting for transfers between devices: 14.1 us -> none  [the longest x1 6.06 us: local(): lax.all_to_all(slot_grad.reshape(source_count, slot_count, feature_count)...]
    dot_general x9 -> x0, matrix products: 8.81 us -> none  [the longest x1 1.35 us: local(): up_part = jnp.dot(token_rows, w_up[0], preferred_element_type=jnp.float32)]
  transfers between devices with their start and end apart: 4 -> 0, of which waited for: 4 -> 0; matrix products, arithmetic and copies ran while one was open for 1% -> 0% of each run, Pallas kernels for 0% -> 0%
where the time goes in v2:
time: 86.7 us; the launch traced here: 86.5 us
  Pallas kernels  85.3 us (98%)
    pallas_call x1, Pallas kernels, local(): pl.pallas_call(kernel, out_shape=(shape((3, ROWS, FF), BF16), shape((2, K...  81.1 us
    pallas_call x1, Pallas kernels, local(): pl.pallas_call(last_kernel, grid=(NB,), out_shape=(shape((D_DEV, TOK), BF...  4.21 us

profile of v2, /device:TPU:1, one launch (start us, length us, event | category | flops | bytes accessed | tf_op | source)
XLA Modules:
  0.0 86.5 jit_solution(5315631221992868177)
XLA Ops:
  0.6 81.1 %shard_map.119 = (bf16[3,192,1536]{2,1,0:T(8,128)(2,1)}, bf16[2,128,192]{2,1,0:T(8,128)(2,1)}, bf16[8,24,128]{2,1,0:T(8,128)(2,1)}, f32[1,3]{1,0:T(1,128)}) custom-call(s32[1,8,24]{2,1,0:T(8,128)} %slots_ref.3, f32[1,192]{1,0:T(1,128)} %prob_ref.1, s32[1,8]{1,0:T(1,128)} %counts_ref.1, bf16[80,1024]{1,0:T(8,128)(2,1)} %bitcast.9, bf16[80,1024]{1,0:T(8,128)(2,1)} %bitcast.10, ...), custom_call_target="tpu_custom_call" | custom-call | tf_op jit(solution)/shard_map/pallas_call | solution.py:367
  81.7 0.0 copy-start
  81.8 4.2 %shard_map.120 = (bf16[80,1024]{1,0:T(8,128)(2,1)}, f32[1,80,1536]{2,1,0:T(8,128)}, f32[1,80,1536]{2,1,0:T(8,128)}, f32[1,80,1536]{2,1,0:T(8,128)}) custom-call(s32[1,8,24]{2,1,0:T(8,128)} %slots_ref.3, bf16[3,192,1536]{2,1,0:T(8,128)(2,1)} %get-tuple-element.13.acts_ref, bf16[2,128,192]{2,1,0:T(8,128)(2,1)} %get-tuple-element.14.rows_ref, ...), custom_call_target="tpu_custom_call" | custom-call | tf_op jit(solution)/shard_map/pallas_call | solution.py:399
  86.0 0.0 copy-done
  86.0 0.5 copy.14
Async XLA Ops:
  81.7 4.2 %copy-start = (f32[1,3]{1,0:T(1,128)S(1)}, f32[1,3]{1,0:T(1,128)}, u32[]{:S(2)}) copy-start(f32[1,3]{1,0:T(1,128)} %get-tuple-element.30) | copy-start | bytes 40

commit v3 on v2

--- a/solution.py
+++ b/solution.py
@@ -20,7 +20,6 @@
 NC = FF // COLS
 TOK = 1024
 SUB = 1
-NB = 4
 NT = (((1,), (1,)), ((), ()))
 
 
@@ -34,8 +33,8 @@
     return jnp.concatenate([tall[:SLOT, e:e + 1] for e in range(EXP)], axis=0)
 
 
-def one_hot(slots_ref, first, width):
-    columns = lax.broadcasted_iota(jnp.int32, (ROWS, width), 1) + first
+def one_hot(slots_ref):
+    columns = lax.broadcasted_iota(jnp.int32, (ROWS, TOK), 1)
     return jnp.where(slot_column(slots_ref) == columns.astype(F32), 1.0, 0.0).astype(BF16)
 
 
@@ -46,11 +45,11 @@
 def kernel(
     slots_ref, prob_ref, counts_ref, tok_ref, grd_ref, wg_ref, wu_ref, wd_ref,
     acts_ref, rows_ref, back_ref, pg_ref,
-    sent, mine, other, weights, part, up_in, down_in, fin_in, own_in, act, acts, rows_t,
+    feats, sent, mine, other, weights, part, up_in, down_in, fin_in, own_in, act, acts, rows_t,
     prob, prob_out, prob_in, back_out, back_in,
     mine_send, mine_recv, other_send, other_recv, w_send, w_recv,
     up_send, up_recv, down_send, down_recv, fin_send, fin_recv, own_send, own_recv,
-    ag_send, ag_recv, pair_send, pair_recv, pr_send, pr_recv, pp_send, pp_recv, back_send, back_recv, out_sem,
+    ag_send, ag_recv, pair_send, pair_recv, pr_send, pr_recv, pp_send, pp_recv, back_send, back_recv, in_sem, out_sem,
 ):
     me = lax.axis_index("fsdp")
     ex = lax.axis_index("expert")
@@ -91,38 +90,55 @@
     for f in friends:
         pl.semaphore_signal(barrier, inc=1, device_id={"fsdp": f, "expert": ex}, device_id_type=MESH)
 
-    table = one_hot(slots_ref, 0, TOK)
-    for i, src in enumerate((tok_ref, grd_ref)):
-        sent[:, i] = pad_features(dot(table, src[...], NT)).reshape(EXP, SLOT, KPAD).astype(BF16)
+    feat_in = [pltpu.make_async_copy(src, feats.at[i], in_sem.at[i]) for i, src in enumerate((tok_ref, grd_ref))]
+    w_in = [
+        pltpu.make_async_copy(src, weights.at[i, pl.ds(0, D_DEV)], in_sem.at[2 + i])
+        for i, src in enumerate((wg_ref, wu_ref, wd_ref))]
+    for copy in feat_in + w_in:
+        copy.start()
+
+    table = one_hot(slots_ref)
+    for i in range(2):
+        feat_in[i].wait()
+        sent[:, i] = pad_features(dot(table, feats[i], NT)).reshape(EXP, SLOT, KPAD).astype(BF16)
     pad = jnp.zeros((KPAD - D_DEV, FF), BF16)
-    for i, w in enumerate((wg_ref, wu_ref, wd_ref)):
-        weights[i, 0:D_DEV] = w[...]
+    for i in range(3):
         weights[i, D_DEV:KPAD] = pad
         weights[i, KPAD + D_DEV:2 * KPAD] = pad
+        w_in[i].wait()
 
     pl.semaphore_wait(barrier, len(friends) + 2 * (EXP - 1))
 
     def peer_expert(k):
         return lax.rem(ex + k, EXP)
 
-    for k in range(EXP):
+    half = ex // 4
+    other_copies = [
+        remote(sent.at[e], other.at[ex], other_send.at[e], other_recv.at[ex], partner, e)
+        for e in (peer_expert(k) for k in range(EXP))]
+
+    @pl.when(half != core)
+    def _():
+        for copy in other_copies:
+            copy.start()
+
+    for k in range(1, EXP):
         e = peer_expert(k)
-        go(remote(sent.at[e], other.at[ex], other_send.at[e], other_recv.at[ex], partner, e))
-        if k:
-            go(remote(sent.at[e], mine.at[ex], mine_send.at[e], mine_recv.at[ex], me, e))
+        go(remote(sent.at[e], mine.at[ex], mine_send.at[e], mine_recv.at[ex], me, e))
     w_copies = [
-        remote(w, weights.at[i, pl.ds(KPAD, D_DEV)], w_send.at[i], w_recv.at[i], partner)
-        for i, w in enumerate((wg_ref, wu_ref, wd_ref))]
+        remote(weights.at[i, pl.ds(0, D_DEV)], weights.at[i, pl.ds(KPAD, D_DEV)], w_send.at[i], w_recv.at[i], partner)
+        for i in range(3)]
     for copy in w_copies:
         go(copy)
     mine[ex] = sent[ex]
     for copy in w_copies:
         copy.wait_recv()
-    for k in range(EXP):
+    for k in range(4):
+        e = 4 * core + k
+        remote(sent.at[e], other.at[e], other_send.at[e], other_recv.at[e], partner, e).wait_recv()
+    for k in range(1, EXP):
         e = peer_expert(k)
-        remote(sent.at[e], other.at[e], other_send.at[e], other_recv.at[e], partner, e).wait_recv()
-        if k:
-            remote(sent.at[e], mine.at[e], mine_send.at[e], mine_recv.at[e], me, e).wait_recv()
+        remote(sent.at[e], mine.at[e], mine_send.at[e], mine_recv.at[e], me, e).wait_recv()
 
     own_rows = [
         jnp.concatenate([
@@ -308,7 +324,7 @@
                 axis=0).astype(BF16)
             acts[i, :, cols] = full
             if i < 2:
-                slot_grad += dot(full, (wg_ref, wu_ref)[i][:, cols], NT)
+                slot_grad += dot(full, weights[i, 0:D_DEV, cols], NT)
     back_out[...] = pad_features(slot_grad).reshape(EXP, SLOT, KPAD).astype(BF16)
     for k in range(1, EXP):
         e = peer_expert(k)
@@ -326,6 +342,11 @@
 
     for copy in pending:
         copy.wait_send()
+
+    @pl.when(half != core)
+    def _():
+        for copy in other_copies:
+            copy.wait_send()
 
     def drain(a, _):
         for q, block in subs:
@@ -350,13 +371,27 @@
     back_out_copy.wait()
 
 
-def last_kernel(slots_ref, acts_ref, rows_ref, back_ref, tg_ref, gg_ref, ug_ref, dg_ref):
-    for i, out in enumerate((gg_ref, ug_ref, dg_ref)):
-        out[0] = dot(rows_ref[i // 2], acts_ref[i])[:D_DEV]
-    back_t = back_ref[...].astype(F32).reshape(ROWS, KPAD).T.astype(BF16)
-    width = TOK // NB
-    table = one_hot(slots_ref, pl.program_id(0) * width, width)
-    tg_ref[...] = dot(back_t, table)[:D_DEV].astype(BF16)
+def last_kernel(slots_ref, acts_ref, rows_ref, back_ref, tg_ref, *refs):
+    grad_refs, (acts, rows, back, tg, grads, in_sem, out_sem) = refs[:3], refs[3:]
+    loads = [pltpu.make_async_copy(rows_ref, rows, in_sem.at[0])]
+    loads += [pltpu.make_async_copy(acts_ref.at[i], acts.at[i], in_sem.at[1 + i]) for i in range(3)]
+    loads += [pltpu.make_async_copy(back_ref, back, in_sem.at[4])]
+    for copy in loads:
+        copy.start()
+    stores = [pltpu.make_async_copy(grads.at[i], grad_refs[i].at[0], out_sem.at[i]) for i in range(3)]
+    stores += [pltpu.make_async_copy(tg, tg_ref, out_sem.at[3])]
+    table = one_hot(slots_ref)
+    loads[0].wait()
+    for i in range(3):
+        loads[1 + i].wait()
+        grads[i] = dot(rows[i // 2], acts[i])[:D_DEV]
+        stores[i].start()
+    loads[4].wait()
+    back_t = back[...].astype(F32).reshape(ROWS, KPAD).T.astype(BF16)
+    tg[...] = dot(back_t, table)[:D_DEV].astype(BF16)
+    stores[3].start()
+    for copy in stores:
+        copy.wait()
 
 
 def local(tokens, out_grad, slot_rows, expert_counts, route_prob, w_gate, w_up, w_down):
@@ -367,9 +402,10 @@
     acts, rows, back, pg = pl.pallas_call(
         kernel,
         out_shape=(shape((3, ROWS, FF), BF16), shape((2, KPAD, ROWS), BF16), shape((EXP, SLOT, KPAD), BF16), shape((1, 3), F32)),
-        in_specs=[vmem] * 8,
+        in_specs=[vmem] * 3 + [hbm] * 5,
         out_specs=(hbm, hbm, hbm, vmem),
         scratch_shapes=[
+            pltpu.VMEM((2, D_DEV, TOK), BF16),
             pltpu.VMEM((EXP, 2, SLOT, KPAD), BF16),
             pltpu.VMEM((EXP, 2, SLOT, KPAD), BF16),
             pltpu.VMEM((EXP, 2, SLOT, KPAD), BF16),
@@ -390,23 +426,24 @@
             dma((EXP,)), dma((EXP,)), dma((EXP,)), dma((EXP,)), dma((3,)), dma((3,)),
             dma((8, 9)), dma((8, 9)), dma((7, 9)), dma((7, 9)), dma((2, 2, 9)), dma((2, 2, 9)), dma((9,)), dma((9,)),
             dma((2, 8, 3)), dma((Z, 3)), dma((Z, 3)), dma((Z, 3)), dma((2, 3)), dma((Z,)), dma, dma,
-            dma((EXP,)), dma((EXP,)), dma((3,)),
+            dma((EXP,)), dma((EXP,)), dma((5,)), dma((3,)),
         ],
         compiler_params=pltpu.CompilerParams(collective_id=0, has_side_effects=True),
     )(slot_rows, route_prob, expert_counts, tokens.T, out_grad.T, w_gate[0], w_up[0], w_down[0])
     grad = shape((1, D_DEV, FF), F32)
-    grad_spec = pl.BlockSpec((1, D_DEV, FF // NB), lambda n: (0, 0, n))
     tg, gg, ug, dg = pl.pallas_call(
         last_kernel,
-        grid=(NB,),
         out_shape=(shape((D_DEV, TOK), BF16), grad, grad, grad),
-        in_specs=[
-            pl.BlockSpec((1, EXP, SLOT), lambda n: (0, 0, 0)),
-            pl.BlockSpec((3, ROWS, FF // NB), lambda n: (0, 0, n)),
-            pl.BlockSpec((2, KPAD, ROWS), lambda n: (0, 0, 0)),
-            pl.BlockSpec((EXP, SLOT, KPAD), lambda n: (0, 0, 0)),
+        in_specs=[vmem, hbm, hbm, hbm],
+        out_specs=(hbm,) * 4,
+        scratch_shapes=[
+            pltpu.VMEM((3, ROWS, FF), BF16),
+            pltpu.VMEM((2, KPAD, ROWS), BF16),
+            pltpu.VMEM((EXP, SLOT, KPAD), BF16),
+            pltpu.VMEM((D_DEV, TOK), BF16),
+            pltpu.VMEM((3, D_DEV, FF), F32),
+            dma((5,)), dma((4,)),
         ],
-        out_specs=(pl.BlockSpec((D_DEV, TOK // NB), lambda n: (0, n)), grad_spec, grad_spec, grad_spec),
     )(slot_rows, acts, rows, back)
     return tg.T, gg, ug, dg, pg
 

time: 86.7 us -> 85.2 us (0.983)
  Pallas kernels: 85.3 us -> 83.8 us
    pallas_call x1, Pallas kernels: 81.1 us -> 80.2 us  [local(): pl.pallas_call(kernel, out_shape=(shape((3, ROWS, FF), BF16), shape((2, K...]
where the time goes in v3:
time: 85.2 us; the launch traced here: 85 us
  Pallas kernels  83.8 us (98%)
    pallas_call x1, Pallas kernels, local(): pl.pallas_call(kernel, out_shape=(shape((3, ROWS, FF), BF16), shape((2, K...  80.2 us
    pallas_call x1, Pallas kernels, local(): pl.pallas_call(last_kernel, out_shape=(shape((D_DEV, TOK), BF16), grad, g...  3.61 us

profile of v3, /device:TPU:1, one launch (start us, length us, event | category | flops | bytes accessed | tf_op | source)
XLA Modules:
  0.0 85.0 jit_solution(1191141831372761923)
XLA Ops:
  0.6 80.2 %shard_map.119 = (bf16[3,192,1536]{2,1,0:T(8,128)(2,1)}, bf16[2,128,192]{2,1,0:T(8,128)(2,1)}, bf16[8,24,128]{2,1,0:T(8,128)(2,1)}, f32[1,3]{1,0:T(1,128)}) custom-call(s32[1,8,24]{2,1,0:T(8,128)} %slots_ref.3, f32[1,192]{1,0:T(1,128)} %prob_ref.1, s32[1,8]{1,0:T(1,128)} %counts_ref.1, bf16[80,1024]{1,0:T(8,128)(2,1)} %bitcast.9, bf16[80,1024]{1,0:T(8,128)(2,1)} %bitcast.10, ...), custom_call_target="tpu_custom_call" | custom-call | tf_op jit(solution)/shard_map/pallas_call | solution.py:402
  80.8 0.0 copy-start
  80.8 3.6 %shard_map.120 = (bf16[80,1024]{1,0:T(8,128)(2,1)}, f32[1,80,1536]{2,1,0:T(8,128)}, f32[1,80,1536]{2,1,0:T(8,128)}, f32[1,80,1536]{2,1,0:T(8,128)}) custom-call(s32[1,8,24]{2,1,0:T(8,128)} %slots_ref.3, bf16[3,192,1536]{2,1,0:T(8,128)(2,1)} %get-tuple-element.13.acts_ref, bf16[2,128,192]{2,1,0:T(8,128)(2,1)} %get-tuple-element.14.rows_ref, ...), custom_call_target="tpu_custom_call" | custom-call | tf_op jit(solution)/shard_map/pallas_call | solution.py:434
  84.4 0.0 copy-done
  84.4 0.5 copy.14
Async XLA Ops:
  80.8 3.6 %copy-start = (f32[1,3]{1,0:T(1,128)S(1)}, f32[1,3]{1,0:T(1,128)}, u32[]{:S(2)}) copy-start(f32[1,3]{1,0:T(1,128)} %get-tuple-element.30) | copy-start | bytes 40

commit v4 on v3

--- a/solution.py
+++ b/solution.py
@@ -45,11 +45,11 @@
 def kernel(
     slots_ref, prob_ref, counts_ref, tok_ref, grd_ref, wg_ref, wu_ref, wd_ref,
     acts_ref, rows_ref, back_ref, pg_ref,
-    feats, sent, mine, other, weights, part, up_in, down_in, fin_in, own_in, act, acts, rows_t,
+    feats, sent, mine, other, weights, part, up_in, down_in, fin_in, own_in, act,
     prob, prob_out, prob_in, back_out, back_in,
     mine_send, mine_recv, other_send, other_recv, w_send, w_recv,
     up_send, up_recv, down_send, down_recv, fin_send, fin_recv, own_send, own_recv,
-    ag_send, ag_recv, pair_send, pair_recv, pr_send, pr_recv, pp_send, pp_recv, back_send, back_recv, in_sem, out_sem,
+    ag_send, ag_recv, pair_send, pair_recv, pr_send, pr_recv, pp_send, pp_recv, back_send, back_recv, in_sem,
 ):
     me = lax.axis_index("fsdp")
     ex = lax.axis_index("expert")
@@ -70,16 +70,13 @@
     cross = [at_z(wrap(z + d), 1 - y), at_z(wrap(z - d), 1 - y)]
     y_peer = at_z(z, 1 - y)
     sign = (d, -d)
-    pending = []
-
     def remote(src, dst, send, recv, f, e=None):
         return pltpu.make_async_remote_copy(
             src_ref=src, dst_ref=dst, send_sem=send, recv_sem=recv,
             device_id={"fsdp": f, "expert": ex if e is None else e}, device_id_type=MESH)
 
-    def go(copy):
-        copy.start()
-        pending.append(copy)
+    def sent_all(ref, sem):
+        remote(ref, ref, sem, sem, partner).wait_send()
 
     barrier = pltpu.get_barrier_semaphore()
     friends = [partner, y_peer] + near + far + cross
@@ -114,7 +111,7 @@
 
     half = ex // 4
     other_copies = [
-        remote(sent.at[e], other.at[ex], other_send.at[e], other_recv.at[ex], partner, e)
+        remote(sent.at[e], other.at[ex], other_send, other_recv.at[ex], partner, e)
         for e in (peer_expert(k) for k in range(EXP))]
 
     @pl.when(half != core)
@@ -122,23 +119,38 @@
         for copy in other_copies:
             copy.start()
 
-    for k in range(1, EXP):
-        e = peer_expert(k)
-        go(remote(sent.at[e], mine.at[ex], mine_send.at[e], mine_recv.at[ex], me, e))
+    mine_copies = [
+        remote(sent.at[e], mine.at[ex], mine_send, mine_recv.at[ex], me, e)
+        for e in (peer_expert(k) for k in range(1, EXP))]
+
+    @pl.when(half == core)
+    def _():
+        for copy in mine_copies:
+            copy.start()
+
     w_copies = [
-        remote(weights.at[i, pl.ds(0, D_DEV)], weights.at[i, pl.ds(KPAD, D_DEV)], w_send.at[i], w_recv.at[i], partner)
+        remote(weights.at[i, pl.ds(0, D_DEV)], weights.at[i, pl.ds(KPAD, D_DEV)], w_send, w_recv.at[i], partner)
         for i in range(3)]
     for copy in w_copies:
-        go(copy)
+        copy.start()
     mine[ex] = sent[ex]
     for copy in w_copies:
         copy.wait_recv()
+
+    def mine_wait(e):
+        @pl.when(e != ex)
+        def _():
+            remote(sent.at[e], mine.at[e], mine_send, mine_recv.at[e], me, e).wait_recv()
+
     for k in range(4):
         e = 4 * core + k
-        remote(sent.at[e], other.at[e], other_send.at[e], other_recv.at[e], partner, e).wait_recv()
-    for k in range(1, EXP):
-        e = peer_expert(k)
-        remote(sent.at[e], mine.at[e], mine_send.at[e], mine_recv.at[e], me, e).wait_recv()
+        remote(sent.at[e], other.at[e], other_send, other_recv.at[e], partner, e).wait_recv()
+        mine_wait(e)
+
+    @pl.when(half != core)
+    def _():
+        for copy in mine_copies:
+            copy.start()
 
     own_rows = [
         jnp.concatenate([
@@ -157,18 +169,18 @@
     subs = [(q, pl.ds(q, SUB)) for q in range(0, 9, SUB)]
 
     def up_copy(a, q, block, src, skip=False):
-        return remote(src, up_in.at[a - 1, block], up_send.at[a - 1, q], up_recv.at[a - 1, q], far[0] if skip else near[0])
+        return remote(src, up_in.at[a - 1, block], up_send, up_recv.at[a - 1, q], far[0] if skip else near[0])
 
     def down_copy(a, q, block, src):
-        return remote(src, down_in.at[a - 1, block], down_send.at[a - 1, q], down_recv.at[a - 1, q], near[1])
+        return remote(src, down_in.at[a - 1, block], down_send, down_recv.at[a - 1, q], near[1])
 
     def fin_copy(way, other_plane, q, block, src):
         f = (cross if other_plane else near)[way]
-        return remote(src, fin_in.at[way, other_plane, block], fin_send.at[way, other_plane, q],
+        return remote(src, fin_in.at[way, other_plane, block], fin_send,
                       fin_recv.at[way, other_plane, q], f)
 
     def own_copy(q, block):
-        return remote(part.at[z, block], own_in.at[block], own_send.at[q], own_recv.at[q], y_peer)
+        return remote(part.at[z, block], own_in.at[block], own_send, own_recv.at[q], y_peer)
 
     for q, block in subs:
         up_copy(8, q, block, part.at[wrap(z + 8 * d), block], True).start()
@@ -177,10 +189,10 @@
     for q, block in subs:
         own_copy(q, block).start()
 
+    for k in range(4):
+        mine_wait(4 * (1 - core) + k)
     for i in range(2):
-        rows_t[i] = mine[:, i].astype(F32).reshape(ROWS, KPAD).T.astype(BF16)
-    rows_out = pltpu.make_async_copy(rows_t, rows_ref, out_sem.at[0])
-    rows_out.start()
+        rows_ref[i] = mine[:, i].astype(F32).reshape(ROWS, KPAD).T.astype(BF16)
 
     def up_add(j, q, block):
         up_copy(j + 1, q, block, up_in.at[j, block]).wait_recv()
@@ -225,19 +237,19 @@
 
     def ag_copy(way, a, g, two):
         owner = wrap(z - sign[way] * a)
-        return remote(act.at[core, owner, g], act.at[core, owner, g], ag_send.at[way, a + (2 if two else 1) - 1, g],
+        return remote(act.at[core, owner, g], act.at[core, owner, g], ag_send,
                       ag_recv.at[owner, g], (far if two else near)[way])
 
     def ag_arrival(way, a, g):
         owner = wrap(z - sign[way] * a)
-        return remote(act.at[core, owner, g], act.at[core, owner, g], ag_send.at[way, 0, g], ag_recv.at[owner, g], near[way])
-
-    def pair_copy(half, owner, g):
-        return remote(act.at[half, owner, g], act.at[half, owner, g], pair_send.at[owner, g], pair_recv.at[owner, g], partner)
+        return remote(act.at[core, owner, g], act.at[core, owner, g], ag_send, ag_recv.at[owner, g], near[way])
+
+    def pair_copy(owner, g):
+        return remote(act.at[core, owner, g], act.at[core, owner, g], pair_send, pair_recv, partner)
 
     def pr_copy(way, a, two):
         owner = wrap(z - sign[way] * a)
-        return remote(prob.at[owner], prob.at[owner], pr_send.at[way, a + (2 if two else 1) - 1], pr_recv.at[owner],
+        return remote(prob.at[owner], prob.at[owner], pr_send, pr_recv.at[owner],
                       (far if two else near)[way])
 
     last = (8, 7)
@@ -246,7 +258,7 @@
         for two in (True, False):
             for way in range(2):
                 if a + (2 if two else 1) <= last[way]:
-                    go(ag_copy(way, a, g, two))
+                    ag_copy(way, a, g, two).start()
 
     tile = jnp.zeros((8, 128), F32)
     for g in range(3):
@@ -275,12 +287,12 @@
         act[core, z, g, 1] = (hidden_grad * silu).astype(BF16)
         act[core, z, g, 2] = (hidden * scale).astype(BF16)
         hand_on(0, g)
-        go(pair_copy(core, z, g))
+        pair_copy(z, g).start()
         tile += jnp.where(spot == g, live * jnp.sum(hidden * down, axis=1, keepdims=True), 0.0)
     prob[z] = tile
     for way in range(2):
         for two in (True, False):
-            go(pr_copy(way, 0, two))
+            pr_copy(way, 0, two).start()
 
     for t in range(1, 5):
         for g in range(3):
@@ -290,15 +302,26 @@
             hand_on(2 * t, g)
             for way in range(2):
                 if 2 * t <= last[way]:
-                    go(pair_copy(core, wrap(z - sign[way] * 2 * t), g))
+                    pair_copy(wrap(z - sign[way] * 2 * t), g).start()
         for g in range(3):
             for way in range(2):
                 ag_arrival(way, 2 * t - 1, g).wait_recv()
-                go(pair_copy(core, wrap(z - sign[way] * (2 * t - 1)), g))
+                pair_copy(wrap(z - sign[way] * (2 * t - 1)), g).start()
         if t == 1:
+            sent_all(part.at[pl.ds(0, 7)], up_send)
+            sent_all(part.at[pl.ds(0, 6)], down_send)
+            sent_all(part.at[pl.ds(0, 4)], fin_send)
+            sent_all(part.at[0], own_send)
+            sent_all(sent.at[pl.ds(0, EXP - 1)], mine_send)
+            sent_all(weights.at[pl.ds(0, 3), pl.ds(0, D_DEV)], w_send)
+
+            @pl.when(half != core)
+            def _():
+                sent_all(sent, other_send)
+
             for way in range(2):
                 pr_copy(way, 2, False).wait_recv()
-                go(pr_copy(way, 2, False))
+                pr_copy(way, 2, False).start()
                 pr_copy(way, 1, False).wait_recv()
         if t == 2:
             for way in range(2):
@@ -306,14 +329,9 @@
             group = z // NC
             prob_out[...] = sum(prob[group * NC + c] for c in range(NC))
             pp = remote(prob_out, prob_in, pp_send, pp_recv, partner)
-            go(pp)
-
-    def pair_wait(owner, _):
-        for g in range(3):
-            pair_copy(1 - core, owner, g).wait_recv()
-        return 0
-
-    lax.fori_loop(0, Z, pair_wait, 0)
+            pp.start()
+
+    remote(act.at[1 - core], act.at[1 - core], pair_send, pair_recv, partner).wait_recv()
 
     slot_grad = jnp.zeros((ROWS, D_DEV), F32)
     for c in range(NC):
@@ -322,15 +340,13 @@
             full = jnp.concatenate(
                 [act[h, r * NC + c, g, i].astype(F32) for h in range(2) for r in range(4) for g in range(3)],
                 axis=0).astype(BF16)
-            acts[i, :, cols] = full
+            acts_ref[i, :, cols] = full
             if i < 2:
                 slot_grad += dot(full, weights[i, 0:D_DEV, cols], NT)
     back_out[...] = pad_features(slot_grad).reshape(EXP, SLOT, KPAD).astype(BF16)
     for k in range(1, EXP):
         e = peer_expert(k)
-        go(remote(back_out.at[e], back_in.at[ex], back_send.at[e], back_recv.at[ex], me, e))
-    acts_out = pltpu.make_async_copy(acts, acts_ref, out_sem.at[1])
-    acts_out.start()
+        remote(back_out.at[e], back_in.at[ex], back_send, back_recv.at[ex], me, e).start()
     back_in[ex] = back_out[ex]
 
     pp.wait_recv()
@@ -340,55 +356,27 @@
     picked = [jnp.sum(jnp.where(place == first + j, total, 0.0), axis=(0, 1), keepdims=True) for j in range(3)]
     pg_ref[...] = jnp.concatenate(picked, axis=1)
 
-    for copy in pending:
-        copy.wait_send()
-
-    @pl.when(half != core)
-    def _():
-        for copy in other_copies:
-            copy.wait_send()
-
-    def drain(a, _):
-        for q, block in subs:
-            up_copy(a, q, block, up_in.at[a - 1, block]).wait_send()
-            down_copy(a, q, block, down_in.at[a - 1, block]).wait_send()
-        return 0
-
-    lax.fori_loop(2, 8, drain, 0)
-    for q, block in subs:
-        up_copy(8, q, block, up_in.at[7, block], True).wait_send()
-        own_copy(q, block).wait_send()
-        for way in range(2):
-            for other_plane in range(2):
-                fin_copy(way, other_plane, q, block, fin_in.at[way, other_plane, block]).wait_send()
+    sent_all(act.at[core, pl.ds(0, 15)], ag_send)
+    sent_all(act.at[core], pair_send)
+    sent_all(prob.at[pl.ds(0, 6)], pr_send)
+    sent_all(prob_out, pp_send)
+    sent_all(back_out.at[pl.ds(0, EXP - 1)], back_send)
     for k in range(1, EXP):
         e = peer_expert(k)
-        remote(back_out.at[e], back_in.at[e], back_send.at[e], back_recv.at[e], me, e).wait_recv()
-    back_out_copy = pltpu.make_async_copy(back_in, back_ref, out_sem.at[2])
-    back_out_copy.start()
-    rows_out.wait()
-    acts_out.wait()
-    back_out_copy.wait()
-
-
-def last_kernel(slots_ref, acts_ref, rows_ref, back_ref, tg_ref, *refs):
-    grad_refs, (acts, rows, back, tg, grads, in_sem, out_sem) = refs[:3], refs[3:]
-    loads = [pltpu.make_async_copy(rows_ref, rows, in_sem.at[0])]
-    loads += [pltpu.make_async_copy(acts_ref.at[i], acts.at[i], in_sem.at[1 + i]) for i in range(3)]
-    loads += [pltpu.make_async_copy(back_ref, back, in_sem.at[4])]
-    for copy in loads:
-        copy.start()
+        remote(back_out.at[e], back_in.at[e], back_send, back_recv.at[e], me, e).wait_recv()
+    back_ref[...] = back_in[...]
+
+
+def last_kernel(slots_ref, acts_ref, rows_ref, back_ref, pg_in, tg_ref, gg_ref, ug_ref, dg_ref, pg_ref, tg, grads, out_sem):
+    grad_refs = (gg_ref, ug_ref, dg_ref)
     stores = [pltpu.make_async_copy(grads.at[i], grad_refs[i].at[0], out_sem.at[i]) for i in range(3)]
     stores += [pltpu.make_async_copy(tg, tg_ref, out_sem.at[3])]
-    table = one_hot(slots_ref)
-    loads[0].wait()
     for i in range(3):
-        loads[1 + i].wait()
-        grads[i] = dot(rows[i // 2], acts[i])[:D_DEV]
+        grads[i] = dot(rows_ref[i // 2], acts_ref[i])[:D_DEV]
         stores[i].start()
-    loads[4].wait()
-    back_t = back[...].astype(F32).reshape(ROWS, KPAD).T.astype(BF16)
-    tg[...] = dot(back_t, table)[:D_DEV].astype(BF16)
+    pg_ref[...] = pg_in[...]
+    back_t = back_ref[...].astype(F32).reshape(ROWS, KPAD).T.astype(BF16)
+    tg[...] = dot(back_t, one_hot(slots_ref))[:D_DEV].astype(BF16)
     stores[3].start()
     for copy in stores:
         copy.wait()
@@ -401,9 +389,11 @@
     shape = jax.ShapeDtypeStruct
     acts, rows, back, pg = pl.pallas_call(
         kernel,
-        out_shape=(shape((3, ROWS, FF), BF16), shape((2, KPAD, ROWS), BF16), shape((EXP, SLOT, KPAD), BF16), shape((1, 3), F32)),
+        out_shape=(
+            pltpu.VMEM((3, ROWS, FF), BF16), pltpu.VMEM((2, KPAD, ROWS), BF16), pltpu.VMEM((EXP, SLOT, KPAD), BF16),
+            pltpu.VMEM((1, 3), F32)),
         in_specs=[vmem] * 3 + [hbm] * 5,
-        out_specs=(hbm, hbm, hbm, vmem),
+        out_specs=(vmem,) * 4,
         scratch_shapes=[
             pltpu.VMEM((2, D_DEV, TOK), BF16),
             pltpu.VMEM((EXP, 2, SLOT, KPAD), BF16),
@@ -416,35 +406,25 @@
             pltpu.VMEM((2, 2, 9, 8, COLS), F32),
             pltpu.VMEM((9, 8, COLS), F32),
             pltpu.VMEM((2, Z, 3, 3, 8, COLS), BF16),
-            pltpu.VMEM((3, ROWS, FF), BF16),
-            pltpu.VMEM((2, KPAD, ROWS), BF16),
             pltpu.VMEM((Z, 8, 128), F32),
             pltpu.VMEM((8, 128), F32),
             pltpu.VMEM((8, 128), F32),
             pltpu.VMEM((EXP, SLOT, KPAD), BF16),
             pltpu.VMEM((EXP, SLOT, KPAD), BF16),
-            dma((EXP,)), dma((EXP,)), dma((EXP,)), dma((EXP,)), dma((3,)), dma((3,)),
-            dma((8, 9)), dma((8, 9)), dma((7, 9)), dma((7, 9)), dma((2, 2, 9)), dma((2, 2, 9)), dma((9,)), dma((9,)),
-            dma((2, 8, 3)), dma((Z, 3)), dma((Z, 3)), dma((Z, 3)), dma((2, 3)), dma((Z,)), dma, dma,
-            dma((EXP,)), dma((EXP,)), dma((5,)), dma((3,)),
+            dma, dma((EXP,)), dma, dma((EXP,)), dma, dma((3,)),
+            dma, dma((8, 9)), dma, dma((7, 9)), dma, dma((2, 2, 9)), dma, dma((9,)),
+            dma, dma((Z, 3)), dma, dma, dma, dma((Z,)), dma, dma, dma, dma((EXP,)), dma((5,)),
         ],
         compiler_params=pltpu.CompilerParams(collective_id=0, has_side_effects=True),
     )(slot_rows, route_prob, expert_counts, tokens.T, out_grad.T, w_gate[0], w_up[0], w_down[0])
     grad = shape((1, D_DEV, FF), F32)
-    tg, gg, ug, dg = pl.pallas_call(
+    tg, gg, ug, dg, pg = pl.pallas_call(
         last_kernel,
-        out_shape=(shape((D_DEV, TOK), BF16), grad, grad, grad),
-        in_specs=[vmem, hbm, hbm, hbm],
-        out_specs=(hbm,) * 4,
-        scratch_shapes=[
-            pltpu.VMEM((3, ROWS, FF), BF16),
-            pltpu.VMEM((2, KPAD, ROWS), BF16),
-            pltpu.VMEM((EXP, SLOT, KPAD), BF16),
-            pltpu.VMEM((D_DEV, TOK), BF16),
-            pltpu.VMEM((3, D_DEV, FF), F32),
-            dma((5,)), dma((4,)),
-        ],
-    )(slot_rows, acts, rows, back)
+        out_shape=(shape((D_DEV, TOK), BF16), grad, grad, grad, shape((1, 3), F32)),
+        in_specs=[vmem] * 5,
+        out_specs=(hbm,) * 4 + (vmem,),
+        scratch_shapes=[pltpu.VMEM((D_DEV, TOK), BF16), pltpu.VMEM((3, D_DEV, FF), F32), dma((4,))],
+    )(slot_rows, acts, rows, back, pg)
     return tg.T, gg, ug, dg, pg
 
 

time: 85.2 us -> 81.6 us (0.958)
  Pallas kernels: 83.8 us -> 77.7 us
  local copies, waits for them, and re-layouts: 0.52 us -> 2.98 us
    pallas_call x1, Pallas kernels: 80.2 us -> 74.3 us  [local(): pl.pallas_call(kernel, out_shape=(pltpu.VMEM((3, ROWS, FF), BF16), pltpu....]
    unnamed x3 -> x8, local copies, waits for them, and re-layouts: 0.52 us -> 2.98 us
where the time goes in v4:
time: 81.6 us; the launch traced here: 81.4 us
  Pallas kernels  77.7 us (95%)
  local copies, waits for them, and re-layouts  2.98 us (4%)
    pallas_call x1, Pallas kernels, local(): pl.pallas_call(kernel, out_shape=(pltpu.VMEM((3, ROWS, FF), BF16), pltpu....  74.3 us
    pallas_call x1, Pallas kernels, local(): pl.pallas_call(last_kernel, out_shape=(shape((D_DEV, TOK), BF16), grad, g...  3.43 us
    unnamed x8, local copies, waits for them, and re-layouts  2.98 us

profile of v4, /device:TPU:1, one launch (start us, length us, event | category | flops | bytes accessed | tf_op | source)
XLA Modules:
  0.0 81.4 jit_solution(6173528297769415147)
XLA Ops:
  0.6 74.3 %shard_map.119 = (bf16[3,192,1536]{2,1,0:T(8,128)(2,1)S(1)}, bf16[2,128,192]{2,1,0:T(8,128)(2,1)S(1)}, bf16[8,24,128]{2,1,0:T(8,128)(2,1)S(1)}, f32[1,3]{1,0:T(1,128)S(1)}) custom-call(s32[1,8,24]{2,1,0:T(8,128)} %slots_ref.3, f32[1,192]{1,0:T(1,128)} %prob_ref.1, s32[1,8]{1,0:T(1,128)} %counts_ref.1, bf16[80,1024]{1,0:T(8,128)(2,1)} %bitcast.9, ...), custom_call_target="tpu_custom_call" | custom-call | tf_op jit(solution)/shard_map/pallas_call | solution.py:390
  74.9 0.0 copy-start
  75.0 1.2 %copy-done = bf16[3,192,1536]{2,1,0:T(8,128)(2,1)} copy-done((bf16[3,192,1536]{2,1,0:T(8,128)(2,1)}, bf16[3,192,1536]{2,1,0:T(8,128)(2,1)S(1)}, u32[]{:S(2)}) %copy-start) | copy-done | bytes 1769496
  76.2 0.0 copy-start.1
  76.2 0.6 copy-done.1
  76.8 0.0 copy-start.2
  76.8 0.6 copy-done.2
  77.5 0.0 copy-start.3
  77.5 0.5 copy-done.3
  77.9 3.4 %shard_map.120 = (bf16[80,1024]{1,0:T(8,128)(2,1)}, f32[1,80,1536]{2,1,0:T(8,128)}, f32[1,80,1536]{2,1,0:T(8,128)}, f32[1,80,1536]{2,1,0:T(8,128)}, f32[1,3]{1,0:T(1,128)}) custom-call(s32[1,8,24]{2,1,0:T(8,128)} %slots_ref.3, bf16[3,192,1536]{2,1,0:T(8,128)(2,1)} %copy-done, bf16[2,128,192]{2,1,0:T(8,128)(2,1)} %copy-done.1, bf16[8,24,128]{2,1,0:T(8,128)(2,1)} %copy-done.2, ...), custom_call_target="tpu_custom_call" | custom-call | tf_op jit(solution)/shard_map/pallas_call | solution.py:421
Async XLA Ops:
  74.9 1.2 %copy-start = (bf16[3,192,1536]{2,1,0:T(8,128)(2,1)}, bf16[3,192,1536]{2,1,0:T(8,128)(2,1)S(1)}, u32[]{:S(2)}) copy-start(bf16[3,192,1536]{2,1,0:T(8,128)(2,1)S(1)} %get-tuple-element.14.acts_ref) | copy-start | bytes 5308420
  76.2 0.6 copy-start.1
  76.8 0.6 copy-start.2
  77.5 0.5 copy-start.3

commit v5 on v4

--- a/solution.py
+++ b/solution.py
@@ -424,7 +424,7 @@
         in_specs=[vmem] * 5,
         out_specs=(hbm,) * 4 + (vmem,),
         scratch_shapes=[pltpu.VMEM((D_DEV, TOK), BF16), pltpu.VMEM((3, D_DEV, FF), F32), dma((4,))],
-    )(slot_rows, acts, rows, back, pg)
+    )(slot_rows, *(pltpu.with_memory_space_constraint(a, pltpu.VMEM) for a in (acts, rows, back, pg)))
     return tg.T, gg, ug, dg, pg
 
 

time: 81.6 us -> 77.8 us (0.953)
  local copies, waits for them, and re-layouts: 2.98 us -> 0 us
    unnamed x8 -> x0, local copies, waits for them, and re-layouts: 2.98 us -> none
where the time goes in v5:
time: 77.8 us; the launch traced here: 77.6 us
  Pallas kernels  76.9 us (99%)
    pallas_call x1, Pallas kernels, local(): pl.pallas_call(kernel, out_shape=(pltpu.VMEM((3, ROWS, FF), BF16), pltpu....  74.3 us
    pallas_call x1, Pallas kernels, local(): pl.pallas_call(last_kernel, out_shape=(shape((D_DEV, TOK), BF16), grad, g...  2.64 us

profile of v5, /device:TPU:1, one launch (start us, length us, event | category | flops | bytes accessed | tf_op | source)
XLA Modules:
  0.0 77.6 jit_solution(6301497065731003105)
XLA Ops:
  0.6 74.3 %shard_map.119 = (bf16[3,192,1536]{2,1,0:T(8,128)(2,1)S(1)}, bf16[2,128,192]{2,1,0:T(8,128)(2,1)S(1)}, bf16[8,24,128]{2,1,0:T(8,128)(2,1)S(1)}, f32[1,3]{1,0:T(1,128)S(1)}) custom-call(s32[1,8,24]{2,1,0:T(8,128)} %slots_ref.3, f32[1,192]{1,0:T(1,128)} %prob_ref.1, s32[1,8]{1,0:T(1,128)} %counts_ref.1, bf16[80,1024]{1,0:T(8,128)(2,1)} %bitcast.9, ...), custom_call_target="tpu_custom_call" | custom-call | tf_op jit(solution)/shard_map/pallas_call | solution.py:390
  74.9 2.6 %shard_map.120 = (bf16[80,1024]{1,0:T(8,128)(2,1)}, f32[1,80,1536]{2,1,0:T(8,128)}, f32[1,80,1536]{2,1,0:T(8,128)}, f32[1,80,1536]{2,1,0:T(8,128)}, f32[1,3]{1,0:T(1,128)}) custom-call(s32[1,8,24]{2,1,0:T(8,128)} %slots_ref.3, bf16[3,192,1536]{2,1,0:T(8,128)(2,1)S(1)} %get-tuple-element.14.acts_ref, bf16[2,128,192]{2,1,0:T(8,128)(2,1)S(1)} %get-tuple-element.15.rows_ref, ...), custom_call_target="tpu_custom_call" | custom-call | tf_op jit(solution)/shard_map/pallas_call | solution.py:421

commit v6 on v5

--- a/solution.py
+++ b/solution.py
@@ -44,8 +44,8 @@
 
 def kernel(
     slots_ref, prob_ref, counts_ref, tok_ref, grd_ref, wg_ref, wu_ref, wd_ref,
-    acts_ref, rows_ref, back_ref, pg_ref,
-    feats, sent, mine, other, weights, part, up_in, down_in, fin_in, own_in, act,
+    grads_ref, back_ref, pg_ref,
+    feats, sent, mine, other, weights, part, up_in, down_in, fin_in, own_in, act, acts, rows_t,
     prob, prob_out, prob_in, back_out, back_in,
     mine_send, mine_recv, other_send, other_recv, w_send, w_recv,
     up_send, up_recv, down_send, down_recv, fin_send, fin_recv, own_send, own_recv,
@@ -192,7 +192,7 @@
     for k in range(4):
         mine_wait(4 * (1 - core) + k)
     for i in range(2):
-        rows_ref[i] = mine[:, i].astype(F32).reshape(ROWS, KPAD).T.astype(BF16)
+        rows_t[i] = mine[:, i].astype(F32).reshape(ROWS, KPAD).T.astype(BF16)
 
     def up_add(j, q, block):
         up_copy(j + 1, q, block, up_in.at[j, block]).wait_recv()
@@ -340,7 +340,7 @@
             full = jnp.concatenate(
                 [act[h, r * NC + c, g, i].astype(F32) for h in range(2) for r in range(4) for g in range(3)],
                 axis=0).astype(BF16)
-            acts_ref[i, :, cols] = full
+            acts[i, :, cols] = full
             if i < 2:
                 slot_grad += dot(full, weights[i, 0:D_DEV, cols], NT)
     back_out[...] = pad_features(slot_grad).reshape(EXP, SLOT, KPAD).astype(BF16)
@@ -348,6 +348,9 @@
         e = peer_expert(k)
         remote(back_out.at[e], back_in.at[ex], back_send, back_recv.at[ex], me, e).start()
     back_in[ex] = back_out[ex]
+
+    for i in range(3):
+        grads_ref[i] = dot(rows_t[i // 2], acts[i])[:D_DEV]
 
     pp.wait_recv()
     total = jnp.where(core == y, prob_out[...], prob_in[...])
@@ -367,12 +370,10 @@
     back_ref[...] = back_in[...]
 
 
-def last_kernel(slots_ref, acts_ref, rows_ref, back_ref, pg_in, tg_ref, gg_ref, ug_ref, dg_ref, pg_ref, tg, grads, out_sem):
-    grad_refs = (gg_ref, ug_ref, dg_ref)
-    stores = [pltpu.make_async_copy(grads.at[i], grad_refs[i].at[0], out_sem.at[i]) for i in range(3)]
+def last_kernel(slots_ref, grads, back_ref, pg_in, tg_ref, gg_ref, ug_ref, dg_ref, pg_ref, tg, out_sem):
+    stores = [pltpu.make_async_copy(grads.at[i], out.at[0], out_sem.at[i]) for i, out in enumerate((gg_ref, ug_ref, dg_ref))]
     stores += [pltpu.make_async_copy(tg, tg_ref, out_sem.at[3])]
     for i in range(3):
-        grads[i] = dot(rows_ref[i // 2], acts_ref[i])[:D_DEV]
         stores[i].start()
     pg_ref[...] = pg_in[...]
     back_t = back_ref[...].astype(F32).reshape(ROWS, KPAD).T.astype(BF16)
@@ -387,13 +388,12 @@
     hbm = pl.BlockSpec(memory_space=pl.ANY)
     dma = pltpu.SemaphoreType.DMA
     shape = jax.ShapeDtypeStruct
-    acts, rows, back, pg = pl.pallas_call(
+    grads, back, pg = pl.pallas_call(
         kernel,
         out_shape=(
-            pltpu.VMEM((3, ROWS, FF), BF16), pltpu.VMEM((2, KPAD, ROWS), BF16), pltpu.VMEM((EXP, SLOT, KPAD), BF16),
-            pltpu.VMEM((1, 3), F32)),
+            pltpu.VMEM((3, D_DEV, FF), F32), pltpu.VMEM((EXP, SLOT, KPAD), BF16), pltpu.VMEM((1, 3), F32)),
         in_specs=[vmem] * 3 + [hbm] * 5,
-        out_specs=(vmem,) * 4,
+        out_specs=(vmem,) * 3,
         scratch_shapes=[
             pltpu.VMEM((2, D_DEV, TOK), BF16),
             pltpu.VMEM((EXP, 2, SLOT, KPAD), BF16),
@@ -406,6 +406,8 @@
             pltpu.VMEM((2, 2, 9, 8, COLS), F32),
             pltpu.VMEM((9, 8, COLS), F32),
             pltpu.VMEM((2, Z, 3, 3, 8, COLS), BF16),
+            pltpu.VMEM((3, ROWS, FF), BF16),
+            pltpu.VMEM((2, KPAD, ROWS), BF16),
             pltpu.VMEM((Z, 8, 128), F32),
             pltpu.VMEM((8, 128), F32),
             pltpu.VMEM((8, 128), F32),
@@ -421,10 +423,10 @@
     tg, gg, ug, dg, pg = pl.pallas_call(
         last_kernel,
         out_shape=(shape((D_DEV, TOK), BF16), grad, grad, grad, shape((1, 3), F32)),
-        in_specs=[vmem] * 5,
+        in_specs=[vmem] * 4,
         out_specs=(hbm,) * 4 + (vmem,),
-        scratch_shapes=[pltpu.VMEM((D_DEV, TOK), BF16), pltpu.VMEM((3, D_DEV, FF), F32), dma((4,))],
-    )(slot_rows, *(pltpu.with_memory_space_constraint(a, pltpu.VMEM) for a in (acts, rows, back, pg)))
+        scratch_shapes=[pltpu.VMEM((D_DEV, TOK), BF16), dma((4,))],
+    )(slot_rows, *(pltpu.with_memory_space_constraint(a, pltpu.VMEM) for a in (grads, back, pg)))
     return tg.T, gg, ug, dg, pg
 
 

time: 77.8 us -> 77.5 us (level)
  no operation moved by 1% of the time
where the time goes in v6:
time: 77.5 us; the launch traced here: 77.3 us
  Pallas kernels  76.7 us (99%)
    pallas_call x1, Pallas kernels, local(): pl.pallas_call(kernel, out_shape=(pltpu.VMEM((3, D_DEV, FF), F32), pltpu....  74.3 us
    pallas_call x1, Pallas kernels, local(): pl.pallas_call(last_kernel, out_shape=(shape((D_DEV, TOK), BF16), grad, g...  2.39 us

profile of v6, /device:TPU:1, one launch (start us, length us, event | category | flops | bytes accessed | tf_op | source)
XLA Modules:
  0.0 77.3 jit_solution(378725795735602929)
XLA Ops:
  0.6 74.3 %shard_map.119 = (f32[3,80,1536]{2,1,0:T(8,128)S(1)}, bf16[8,24,128]{2,1,0:T(8,128)(2,1)S(1)}, f32[1,3]{1,0:T(1,128)S(1)}) custom-call(s32[1,8,24]{2,1,0:T(8,128)} %slots_ref.3, f32[1,192]{1,0:T(1,128)} %prob_ref.1, s32[1,8]{1,0:T(1,128)} %counts_ref.1, bf16[80,1024]{1,0:T(8,128)(2,1)} %bitcast.9, bf16[80,1024]{1,0:T(8,128)(2,1)} %bitcast.10, ...), custom_call_target="tpu_custom_call" | custom-call | tf_op jit(solution)/shard_map/pallas_call | solution.py:391
  74.9 2.4 %shard_map.120 = (bf16[80,1024]{1,0:T(8,128)(2,1)}, f32[1,80,1536]{2,1,0:T(8,128)}, f32[1,80,1536]{2,1,0:T(8,128)}, f32[1,80,1536]{2,1,0:T(8,128)}, f32[1,3]{1,0:T(1,128)}) custom-call(s32[1,8,24]{2,1,0:T(8,128)} %slots_ref.3, f32[3,80,1536]{2,1,0:T(8,128)S(1)} %get-tuple-element.13.grads, bf16[8,24,128]{2,1,0:T(8,128)(2,1)S(1)} %get-tuple-element.14.back_ref, ...), custom_call_target="tpu_custom_call" | custom-call | tf_op jit(solution)/shard_map/pallas_call | solution.py:423
